TPU v7x, 32 devices: a whole 2x2x4 slice. The times are simulated.
32 devices in a mesh: pb: 8 (over y, x, core), ka: 4 (over z).
Axes of the slice: x: 2, y: 2, z: 4, core: 2. Of those that a mesh axis runs over, the one named last changes fastest.
Arguments:
- layer_input: bfloat16 [16384, 768], P(('pb', 'ka')), may hold values from -24 to 24, as said below
- second_start: int32 [8], P('pb'), may hold values from 1024 to 2048, as said below
- gain_attn: float32 [768], replicated, may hold values from 0.5 to 1.5
- w_qkv: bfloat16 [768, 2304], P('ka'), may hold values from -0.21875 to 0.21875
- w_out: bfloat16 [768, 768], P('ka'), may hold values from -3.5 to 3.5
- gain_mlp: float32 [768], replicated, may hold values from 0.5 to 1.5
- w_up: bfloat16 [768, 3072], P('ka'), may hold values from -0.21875 to 0.21875
- w_down: bfloat16 [3072, 768], P('ka'), may hold values from -0.109375 to 0.109375
- d_output: bfloat16 [16384, 768], P(('pb', 'ka')), may hold values from -6 to 6
Outputs:
- output: bfloat16 [16384, 768], P(('pb', 'ka'))
- d_input: float32 [16384, 768], P(('pb', 'ka'))
- d_gain_attn: float32 [768], P('ka')
- d_w_qkv: float32 [768, 2304], P('ka')
- d_w_out: float32 [768, 768], P('ka')
- d_gain_mlp: float32 [768], P('ka')
- d_w_up: float32 [768, 3072], P('ka')
- d_w_down: float32 [3072, 768], P('ka')
- rms: float32 [4], P('ka')
Inputs may be any that keep to these rules, and one draw needn't show every extreme that they name: `layer_input`: every value is finite. `second_start`: exactly half of the 8 groups, drawn from the seed, hold two sequences of 1024 tokens, the second starting at 1024; the others hold one sequence of 2048 tokens and have the value 2048.
All inputs are finite; a program needn't handle non-finite values.
Results may differ from a plain program's by a relative error of at most 0.019.
Values may be sent and summed in bfloat16 or wider, within the bound.
A program may use at most 192 MiB of HBM per device.

v0:
```python
import math

import jax
import jax.numpy as jnp
from jax import lax
from jax.sharding import PartitionSpec as P

D = 768
HEADS = 12
HEAD = 64


def normalize(values):
    center = values - jnp.mean(values, axis=1, keepdims=True)
    spread = jnp.mean(center * center, axis=1, keepdims=True)
    return center * lax.rsqrt(spread + 1e-05)


def norm_gain(values, gain_vec):
    return normalize(values) * gain_vec


def gelu_tanh(values):
    return jax.nn.gelu(values, approximate=True)


def contract_rows(left, right):
    return lax.dot_general(
        left, right, (((0,), (0,)), ((), ())), preferred_element_type=jnp.float32
    )


def contract_cols(left, right):
    return lax.dot_general(
        left, right, (((1,), (1,)), ((), ())), preferred_element_type=jnp.float32
    )


def body(layer_input, second_start, gain_attn, w_qkv, w_out, gain_mlp, w_up, w_down, d_output):
    row_count = layer_input.shape[0]
    kv_index = lax.axis_index("ka")
    kv_count = lax.axis_size("ka")
    group_rows = row_count * kv_count
    block_rows = min(512, group_rows)
    block_count = group_rows // block_rows
    score_scale = 1.0 / math.sqrt(HEAD)
    split_at = second_start[0]
    full_qkv, full_out, full_up, full_down = (
        lax.all_gather(w_qkv, "ka", axis=0, tiled=True),
        lax.all_gather(w_out, "ka", axis=0, tiled=True),
        lax.all_gather(w_up, "ka", axis=0, tiled=True),
        lax.all_gather(w_down, "ka", axis=0, tiled=True),
    )
    inputs32 = layer_input.astype(jnp.float32)
    attn_in = (normalize(inputs32) * gain_attn).astype(jnp.bfloat16)
    projected = jnp.dot(attn_in, full_qkv, preferred_element_type=jnp.float32).astype(jnp.bfloat16)
    keys_own = projected[:, D : 2 * D].reshape(row_count, HEADS, HEAD)
    values_own = projected[:, 2 * D :].reshape(row_count, HEADS, HEAD)
    block_ids = jnp.arange(block_count)
    own_pos = kv_index * row_count + jnp.arange(row_count)

    def pair_scores(query_blk, query_pos, key_blk, key_pos):
        query_side = query_pos >= split_at
        key_side = key_pos >= split_at
        allowed = (key_pos[None, :] <= query_pos[:, None]) & (
            key_side[None, :] == query_side[:, None]
        )
        scores = (
            jnp.einsum("qhd,khd->hqk", query_blk, key_blk, preferred_element_type=jnp.float32)
            * score_scale
        )
        expo = jnp.where(allowed[None], jnp.cosh(scores), 0.0)
        sine = jnp.where(allowed[None], jnp.sinh(scores), 0.0)
        signed = sine.astype(jnp.bfloat16)
        return (sine, expo, signed)

    def block_scores(query_blk, block_idx):
        query_pos = block_idx * block_rows + jnp.arange(block_rows)
        return pair_scores(query_blk, query_pos, keys_own, own_pos)

    queries_all = lax.all_gather(projected[:, :D], "ka", axis=0, tiled=True)
    query_blocks = queries_all.reshape(block_count, block_rows, HEADS, HEAD)

    def forward_block(pieces):
        query_blk, block_idx = pieces
        sine, expo, signed = block_scores(query_blk, block_idx)
        partial_blk = jnp.einsum(
            "hqk,khd->qhd", signed, values_own, preferred_element_type=jnp.float32
        )
        return (partial_blk.reshape(block_rows, D), jnp.sum(expo, axis=2))

    partial_out, partial_sums = lax.map(forward_block, (query_blocks, block_ids))
    partial_out = partial_out.reshape(group_rows, D)
    partial_sums = jnp.transpose(partial_sums, (1, 0, 2)).reshape(HEADS, group_rows)
    sums_all = lax.psum(partial_sums.astype(jnp.bfloat16), "ka").astype(jnp.float32)
    own_out = lax.psum_scatter(
        partial_out.astype(jnp.bfloat16), "ka", scatter_dimension=0, tiled=True
    ).astype(jnp.float32)
    own_sums = lax.dynamic_slice_in_dim(sums_all, kv_index * row_count, row_count, 1)
    row_totals = own_sums.T[:, :, None]
    attn_heads = own_out.reshape(row_count, HEADS, HEAD) / row_totals
    attn_low = attn_heads.reshape(row_count, D).astype(jnp.bfloat16)
    attn_branch = jnp.dot(attn_low, full_out, preferred_element_type=jnp.float32)
    middle = inputs32 + attn_branch
    mlp_in = (normalize(middle) * gain_mlp).astype(jnp.bfloat16)
    up_proj = jnp.dot(mlp_in, full_up, preferred_element_type=jnp.float32)
    activated = gelu_tanh(up_proj).astype(jnp.bfloat16)
    mlp_branch = jnp.dot(activated, full_down, preferred_element_type=jnp.float32)
    output = (middle + mlp_branch).astype(jnp.bfloat16)
    squares = jnp.stack(
        [
            jnp.sum(inputs32 * inputs32),
            jnp.sum(attn_branch * attn_branch),
            jnp.sum(middle * middle),
            jnp.sum(mlp_branch * mlp_branch),
        ]
    )
    d_act = contract_cols(d_output, full_down)
    d_w_down = contract_rows(activated, d_output)
    gelu_back = jax.vjp(gelu_tanh, up_proj)[1]
    d_up = gelu_back(d_act)[0].astype(jnp.bfloat16)
    d_w_up = contract_rows(mlp_in, d_up)
    d_mlp_in = contract_cols(d_up, full_up)
    norm_back_two = jax.vjp(norm_gain, middle, gain_mlp)[1]
    d_middle_norm, d_gain_mlp = norm_back_two(d_mlp_in)
    d_middle = d_output.astype(jnp.float32) + d_middle_norm
    g_middle = d_middle.astype(jnp.bfloat16)
    d_w_out = contract_rows(attn_low, g_middle)
    d_attn = contract_cols(g_middle, full_out).astype(jnp.bfloat16)
    d_attn_heads = d_attn.astype(jnp.float32).reshape(row_count, HEADS, HEAD)
    d_mixed = (d_attn_heads / row_totals).reshape(row_count, D).astype(jnp.bfloat16)
    row_terms = (jnp.sum(d_attn_heads * attn_heads, axis=2) / own_sums.T).T
    mixed_all, terms_all = (
        lax.all_gather(d_mixed, "ka", axis=0, tiled=True),
        lax.all_gather(row_terms.astype(jnp.bfloat16), "ka", axis=1, tiled=True).astype(
            row_terms.dtype
        ),
    )
    grad_blocks = mixed_all.reshape(block_count, block_rows, HEADS, HEAD)
    term_blocks = jnp.transpose(terms_all.reshape(HEADS, block_count, block_rows), (1, 0, 2))

    def backward_block(carry, pieces):
        key_acc, value_acc = carry
        query_blk, grad_blk, term_blk, block_idx = pieces
        sine, expo, signed = block_scores(query_blk, block_idx)
        d_signed = jnp.einsum(
            "qhd,khd->hqk", grad_blk, values_own, preferred_element_type=jnp.float32
        )
        d_scores = (expo * d_signed - sine * term_blk[:, :, None]).astype(jnp.bfloat16)
        d_query = (
            jnp.einsum("hqk,khd->qhd", d_scores, keys_own, preferred_element_type=jnp.float32)
            * score_scale
        )
        key_acc = (
            key_acc
            + jnp.einsum("hqk,qhd->khd", d_scores, query_blk, preferred_element_type=jnp.float32)
            * score_scale
        )
        value_acc = value_acc + jnp.einsum(
            "hqk,qhd->khd", signed, grad_blk, preferred_element_type=jnp.float32
        )
        return ((key_acc, value_acc), d_query.reshape(block_rows, D))

    zero_acc = jnp.zeros((row_count, HEADS, HEAD), jnp.float32)
    (d_keys, d_values), query_parts = lax.scan(
        backward_block, (zero_acc, zero_acc), (query_blocks, grad_blocks, term_blocks, block_ids)
    )
    d_queries = lax.psum_scatter(
        query_parts.reshape(group_rows, D).astype(jnp.bfloat16),
        "ka",
        scatter_dimension=0,
        tiled=True,
    ).astype(jnp.float32)
    d_projected = jnp.concatenate(
        [d_queries, d_keys.reshape(row_count, D), d_values.reshape(row_count, D)], axis=1
    ).astype(jnp.bfloat16)
    d_w_qkv = contract_rows(attn_in, d_projected)
    d_attn_in = contract_cols(d_projected, full_qkv)
    norm_back_one = jax.vjp(norm_gain, inputs32, gain_attn)[1]
    d_input_norm, d_gain_attn = norm_back_one(d_attn_in)
    d_input = d_middle + d_input_norm
    all_totals = lax.psum(
        (
            lax.psum_scatter(
                d_gain_attn.astype(jnp.bfloat16), "ka", scatter_dimension=0, tiled=True
            ).astype(jnp.float32),
            lax.psum_scatter(
                d_w_qkv.astype(jnp.bfloat16), "ka", scatter_dimension=0, tiled=True
            ).astype(jnp.float32),
            lax.psum_scatter(
                d_w_out.astype(jnp.bfloat16), "ka", scatter_dimension=0, tiled=True
            ).astype(jnp.float32),
            lax.psum_scatter(
                d_gain_mlp.astype(jnp.bfloat16), "ka", scatter_dimension=0, tiled=True
            ).astype(jnp.float32),
            lax.psum_scatter(
                d_w_up.astype(jnp.bfloat16), "ka", scatter_dimension=0, tiled=True
            ).astype(jnp.float32),
            lax.psum_scatter(
                d_w_down.astype(jnp.bfloat16), "ka", scatter_dimension=0, tiled=True
            ).astype(jnp.float32),
            lax.psum_scatter(
                squares.astype(jnp.bfloat16), "ka", scatter_dimension=0, tiled=True
            ).astype(jnp.float32),
        ),
        "pb",
    )
    total_gain_attn, total_qkv, total_out, total_gain_mlp, total_up, total_down, total_squares = (
        all_totals
    )
    entry_count = row_count * kv_count * lax.axis_size("pb") * D
    rms = jnp.sqrt(total_squares / entry_count)
    return (
        output,
        d_input,
        total_gain_attn,
        total_qkv,
        total_out,
        total_gain_mlp,
        total_up,
        total_down,
        rms,
    )


def solution(mesh):
    placed = (
        P(("pb", "ka"), None),
        P("pb"),
        P(),
        P("ka", None),
        P("ka", None),
        P(),
        P("ka", None),
        P("ka", None),
        P(("pb", "ka"), None),
    )
    return jax.shard_map(
        body,
        mesh=mesh,
        in_specs=placed,
        out_specs=(
            P(("pb", "ka"), None),
            P(("pb", "ka"), None),
            P("ka"),
            P("ka", None),
            P("ka", None),
            P("ka"),
            P("ka", None),
            P("ka", None),
            P("ka"),
        ),
        check_vma=False,
    )
```

profile of v0, /device:TPU:0, one launch (start us, length us, event | category | flops | bytes accessed | tf_op | source)
XLA Modules:
  0.0 1237.2 jit_solution(4309461705513859410)
XLA Ops:
  11.4 70.9 %all-gather.7.cloned.1.call-done = bf16[768,2304]{1,0:T(8,128)(2,1)} async-done(((bf16[192,2304]{1,0:T(8,128)(2,1)}), bf16[768,2304]{1,0:T(8,128)(2,1)}) %all-gather.7.cloned.1.call-update) | async-done | bytes 3538960 | tf_op jit(solution)/shard_map/all_gather | solution.py:49
  91.1 58.9 %all-gather.9.cloned.1.call-done = bf16[2048,768]{1,0:T(8,128)(2,1)} async-done(((bf16[512,768]{1,0:T(8,128)(2,1)}), bf16[2048,768]{1,0:T(8,128)(2,1)}) %all-gather.9.cloned.1.call-update) | async-done | bytes 3145744 | tf_op jit(solution)/shard_map/all_gather | solution.py:81
  160.2 100.2 %while.28 = (s32[]{:T(128)}, bf16[4,512,768]{1,2,0:T(8,128)(2,1)}, bf16[4,12,512]{2,1,0:T(8,128)(2,1)S(1)}, s32[4]{0:T(128)S(1)}, s32[]{:T(128)}, /*index=5*/bf1...) while((s32[]{:T(128)}, bf16[4,512,768]{1,2,0:T(8,128)(2,1)}, ...), condition=%wide.region_4.5_spmd.clone, body=%wide.region_2.4_spmd.clone.sunk | while | flops 893907968 | bytes 44357804 | solution.py:92
  171.9 12.4 fusion.127
  197.0 12.4 fusion.127
  222.0 12.4 fusion.127
  247.0 12.4 fusion.127
  274.2 21.6 %psum.56 = bf16[12,2048]{1,0:T(8,128)(2,1)S(1)} all-reduce(bf16[12,2048]{1,0:T(8,128)(2,1)S(1)} %bitcast.147), channel_id=1, replica_groups=mesh['pb'=8,'ka'=4] {'ka'}, use_global_device_ids=true, to_apply=%region_6.7 | all-reduce | flops 24576 | bytes 98304 | tf_op jit(solution)/shard_map/psum | solution.py:95
  297.6 29.0 %reduce-scatter.7.cloned.1.call-done = bf16[512,768]{0,1:T(8,128)(2,1)} async-done(((bf16[2048,768]{0,1:T(8,128)(2,1)}), bf16[512,768]{0,1:T(8,128)(2,1)}) %reduce-scatter.7.cloned.1.call-update) | async-done | bytes 786448 | tf_op jit(solution)/shard_map/reduce_scatter | solution.py:96
  328.8 29.8 %all-gather.11.cloned.1.call-done = bf16[768,768]{1,0:T(8,128)(2,1)} async-done(((bf16[192,768]{1,0:T(8,128)(2,1)}), bf16[768,768]{1,0:T(8,128)(2,1)}) %all-gather.11.cloned.1.call-update) | async-done | bytes 1179664 | tf_op jit(solution)/shard_map/all_gather | solution.py:50
  361.9 86.6 %all-gather.13.cloned.1.call-done = bf16[768,3072]{1,0:T(8,128)(2,1)} async-done(((bf16[192,3072]{1,0:T(8,128)(2,1)}), bf16[768,3072]{1,0:T(8,128)(2,1)}) %all-gather.13.cloned.1.call-update) | async-done | bytes 4718608 | tf_op jit(solution)/shard_map/all_gather | solution.py:51
  448.5 9.0 fusion.56
  461.2 7.9 multiply_reduce_fusion
  477.2 13.6 %all_gather.27 = bf16[12,2048]{1,0:T(8,128)(2,1)S(1)} all-gather(bf16[12,512]{1,0:T(8,128)(2,1)S(1)} %fusion.71), channel_id=1, replica_groups=mesh['pb'=8,'ka'=4] {'ka'}, dimensions={1}, use_global_device_ids=true | all-gather | bytes 61440 | tf_op jit(solution)/shard_map/all_gather | solution.py:135
  490.9 45.4 %all-gather.17.cloned.1.call-done = bf16[2048,768]{1,0:T(8,128)(2,1)} async-done(((bf16[512,768]{1,0:T(8,128)(2,1)}), bf16[2048,768]{1,0:T(8,128)(2,1)}) %all-gather.17.cloned.1.call-update) | async-done | bytes 3145744 | tf_op jit(solution)/shard_map/all_gather | solution.py:134
  551.6 196.9 %while.29 = (s32[]{:T(128)}, f32[512,12,64]{0,2,1:T(8,128)S(1)}, f32[512,12,64]{0,2,1:T(8,128)}, bf16[4,512,768]{2,1,0:T(8,128)(2,1)}, bf16[4,512,12,64]{1,3,2,0...) while((s32[]{:T(128)}, f32[512,12,64]{0,2,1:T(8,128)S(1)}, ...), condition=%wide.region_13.14_spmd.clone, body=%wide.region_12.13_spmd.clone.sunk | while | flops 2148666368 | bytes 137767184 | solution.py:165
  564.1 12.6 %bitcast_add_fusion.5 = f32[512,12,64]{0,2,1:T(8,128)} fusion(f32[512,12,64]{0,2,1:T(8,128)} %get-tuple-element.566, pred[]{:T(512)S(6)} %compare.3, f32[12,512,512]{2,1,0:T(8,128)S(1)} %get-tuple-element.510, pred[512,512]{1,0:T(8,128)(4,1)S(1)} %compare_and_fusion.5, u16[512,512]{1,0:T(8,128)(2,1)S(1)} %get-tuple-element.515, ...), kind=kOutput, calls=%fused_computation.46.clone.1 | convolution fusion | flops 450625536 | bytes 17301508 | tf_op jit(solution)/shard_map/while/body/eval_jaxpr/hqk,qhd->khd/dot_general | solution.py:159
  576.7 16.8 %subtract_convert_fusion.2 = bf16[12,512,512]{2,1,0:T(8,128)(2,1)S(1)} fusion(f32[12,512,512]{2,1,0:T(8,128)} %copy-done.32, f32[12,512]{1,0:T(8,128)S(1)} %bitcast.144, pred[512,512]{1,0:T(8,128)(4,1)S(1)} %compare_and_fusion.5, bf16[512,12,64]{0,2,1:T(8,128)(2,1)} %get-tuple-element.588, u16[512,512]{1,0:T(8,128)(2,1)S(1)} %get-tuple-element.515, ...), kind=kOutput, calls=%fused_computation.39.clone.1 | convolution fusion | flops 465567744 | bytes 21266436 | tf_op jit(solution)/shard_map/while/body/eval_jaxpr/qhd,khd->hqk/dot_general | solution.py:146
  612.5 13.6 %bitcast_add_fusion.5 = f32[512,12,64]{0,2,1:T(8,128)} fusion(f32[512,12,64]{0,2,1:T(8,128)} %get-tuple-element.566, pred[]{:T(512)S(6)} %compare.3, f32[12,512,512]{2,1,0:T(8,128)S(1)} %get-tuple-element.510, pred[512,512]{1,0:T(8,128)(4,1)S(1)} %compare_and_fusion.5, u16[512,512]{1,0:T(8,128)(2,1)S(1)} %get-tuple-element.515, ...), kind=kOutput, calls=%fused_computation.46.clone.1 | convolution fusion | flops 450625536 | bytes 17301508 | tf_op jit(solution)/shard_map/while/body/eval_jaxpr/hqk,qhd->khd/dot_general | solution.py:159
  626.1 16.8 %subtract_convert_fusion.2 = bf16[12,512,512]{2,1,0:T(8,128)(2,1)S(1)} fusion(f32[12,512,512]{2,1,0:T(8,128)} %copy-done.32, f32[12,512]{1,0:T(8,128)S(1)} %bitcast.144, pred[512,512]{1,0:T(8,128)(4,1)S(1)} %compare_and_fusion.5, bf16[512,12,64]{0,2,1:T(8,128)(2,1)} %get-tuple-element.588, u16[512,512]{1,0:T(8,128)(2,1)S(1)} %get-tuple-element.515, ...), kind=kOutput, calls=%fused_computation.39.clone.1 | convolution fusion | flops 465567744 | bytes 21266436 | tf_op jit(solution)/shard_map/while/body/eval_jaxpr/qhd,khd->hqk/dot_general | solution.py:146
  661.9 13.6 %bitcast_add_fusion.5 = f32[512,12,64]{0,2,1:T(8,128)} fusion(f32[512,12,64]{0,2,1:T(8,128)} %get-tuple-element.566, pred[]{:T(512)S(6)} %compare.3, f32[12,512,512]{2,1,0:T(8,128)S(1)} %get-tuple-element.510, pred[512,512]{1,0:T(8,128)(4,1)S(1)} %compare_and_fusion.5, u16[512,512]{1,0:T(8,128)(2,1)S(1)} %get-tuple-element.515, ...), kind=kOutput, calls=%fused_computation.46.clone.1 | convolution fusion | flops 450625536 | bytes 17301508 | tf_op jit(solution)/shard_map/while/body/eval_jaxpr/hqk,qhd->khd/dot_general | solution.py:159
  675.5 16.8 %subtract_convert_fusion.2 = bf16[12,512,512]{2,1,0:T(8,128)(2,1)S(1)} fusion(f32[12,512,512]{2,1,0:T(8,128)} %copy-done.32, f32[12,512]{1,0:T(8,128)S(1)} %bitcast.144, pred[512,512]{1,0:T(8,128)(4,1)S(1)} %compare_and_fusion.5, bf16[512,12,64]{0,2,1:T(8,128)(2,1)} %get-tuple-element.588, u16[512,512]{1,0:T(8,128)(2,1)S(1)} %get-tuple-element.515, ...), kind=kOutput, calls=%fused_computation.39.clone.1 | convolution fusion | flops 465567744 | bytes 21266436 | tf_op jit(solution)/shard_map/while/body/eval_jaxpr/qhd,khd->hqk/dot_general | solution.py:146
  711.3 13.6 %bitcast_add_fusion.5 = f32[512,12,64]{0,2,1:T(8,128)} fusion(f32[512,12,64]{0,2,1:T(8,128)} %get-tuple-element.566, pred[]{:T(512)S(6)} %compare.3, f32[12,512,512]{2,1,0:T(8,128)S(1)} %get-tuple-element.510, pred[512,512]{1,0:T(8,128)(4,1)S(1)} %compare_and_fusion.5, u16[512,512]{1,0:T(8,128)(2,1)S(1)} %get-tuple-element.515, ...), kind=kOutput, calls=%fused_computation.46.clone.1 | convolution fusion | flops 450625536 | bytes 17301508 | tf_op jit(solution)/shard_map/while/body/eval_jaxpr/hqk,qhd->khd/dot_general | solution.py:159
  725.0 16.8 %subtract_convert_fusion.2 = bf16[12,512,512]{2,1,0:T(8,128)(2,1)S(1)} fusion(f32[12,512,512]{2,1,0:T(8,128)} %copy-done.32, f32[12,512]{1,0:T(8,128)S(1)} %bitcast.144, pred[512,512]{1,0:T(8,128)(4,1)S(1)} %compare_and_fusion.5, bf16[512,12,64]{0,2,1:T(8,128)(2,1)} %get-tuple-element.588, u16[512,512]{1,0:T(8,128)(2,1)S(1)} %get-tuple-element.515, ...), kind=kOutput, calls=%fused_computation.39.clone.1 | convolution fusion | flops 465567744 | bytes 21266436 | tf_op jit(solution)/shard_map/while/body/eval_jaxpr/qhd,khd->hqk/dot_general | solution.py:146
  760.3 8.4 convolution_convert_fusion
  772.8 34.7 %reduce-scatter.9.cloned.1.call-done = bf16[512,768]{1,0:T(8,128)(2,1)} async-done(((bf16[2048,768]{1,0:T(8,128)(2,1)}), bf16[512,768]{1,0:T(8,128)(2,1)}) %reduce-scatter.9.cloned.1.call-update) | async-done | bytes 786448 | tf_op jit(solution)/shard_map/reduce_scatter | solution.py:168
  814.8 24.9 %reduce-scatter.13.cloned.1.call-done = bf16[192,768]{1,0:T(8,128)(2,1)} async-done(((bf16[768,768]{1,0:T(8,128)(2,1)}), bf16[192,768]{1,0:T(8,128)(2,1)}) %reduce-scatter.13.cloned.1.call-update) | async-done | bytes 294928 | tf_op jit(solution)/shard_map/reduce_scatter | solution.py:190
  839.7 86.2 %reduce-scatter.15.cloned.1.call-done = bf16[192,3072]{1,0:T(8,128)(2,1)} async-done(((bf16[768,3072]{1,0:T(8,128)(2,1)}), bf16[192,3072]{1,0:T(8,128)(2,1)}) %reduce-scatter.15.cloned.1.call-update) | async-done | bytes 1179664 | tf_op jit(solution)/shard_map/reduce_scatter | solution.py:196
  925.8 88.1 %reduce-scatter.17.cloned.1.call-done = bf16[768,768]{1,0:T(8,128)(2,1)} async-done(((bf16[3072,768]{1,0:T(8,128)(2,1)}), bf16[768,768]{1,0:T(8,128)(2,1)}) %reduce-scatter.17.cloned.1.call-update) | async-done | bytes 1179664 | tf_op jit(solution)/shard_map/reduce_scatter | solution.py:199
  1022.8 11.5 all-reduce.4
  1038.9 44.7 %reduce-scatter.11.cloned.1.call-done = bf16[192,2304]{1,0:T(8,128)(2,1)} async-done(((bf16[768,2304]{1,0:T(8,128)(2,1)}), bf16[192,2304]{1,0:T(8,128)(2,1)}) %reduce-scatter.11.cloned.1.call-update) | async-done | bytes 884752 | tf_op jit(solution)/shard_map/reduce_scatter | solution.py:187
  1083.6 144.7 %all-reduce.6 = (f32[192]{0:T(256)}, f32[192,2304]{1,0:T(8,128)}, f32[192,768]{1,0:T(8,128)}, f32[192]{0:T(256)}, f32[192,3072]{1,0:T(8,128)}, /*index=5*/f32[768,768]{1,0:T(8,128)}, f32[1]{0:T(128)}) all-reduce(f32[192]{0:T(256)S(1)} %get-tuple-element.363, ...), channel_id=1, replica_groups=mesh['pb'=8,'ka'=4] {'pb'}, use_global_device_ids=true, to_apply=%region_19.20 | all-reduce | flops 1769857 | bytes 10619910 | tf_op jit(solution)/shard_map/psum | solution.py:182
  (242 shorter events, 227.8 us)
Async XLA Ops:
  7.2 75.1 %all-gather.7.cloned.1.call-start = ((), (), s32[]{:S(2)}) async-start(), calls=%async_computation.6 | async-start | bytes 4423680 | tf_op jit(solution)/shard_map/all_gather | solution.py:49
  7.9 142.1 %all-gather.9.cloned.1.call-start = ((), (), s32[]{:S(2)}) async-start(), calls=%async_computation.7 | async-start | bytes 3932160 | tf_op jit(solution)/shard_map/all_gather | solution.py:81
  9.3 73.0 %copy-start.13 = (f32[512]{0:T(512)}, f32[512]{0:T(512)S(1)}, u32[]{:S(2)}) copy-start(f32[512]{0:T(512)S(1)} %broadcast_multiply_fusion.1) | copy-start | bytes 6148
  11.4 70.9 %copy-start.15 = (f32[512]{0:T(512)}, f32[512]{0:T(512)S(1)}, u32[]{:S(2)}) copy-start(f32[512]{0:T(512)S(1)} %fusion.72) | copy-start | bytes 6148
  87.8 179.5 %all-gather.15.cloned.1.call-start = ((), (), s32[]{:S(2)}) async-start(), calls=%async_computation.11 | async-start | bytes 5898240 | tf_op jit(solution)/shard_map/all_gather | solution.py:52
  88.5 238.1 %reduce-scatter.7.cloned.1.call-start = ((), (), s32[]{:S(2)}) async-start(), calls=%async_computation.8 | async-start | bytes 3932160 | tf_op jit(solution)/shard_map/reduce_scatter | solution.py:96
  265.6 93.0 %all-gather.11.cloned.1.call-start = ((), (), s32[]{:S(2)}) async-start(), calls=%async_computation.9 | async-start | bytes 1474560 | tf_op jit(solution)/shard_map/all_gather | solution.py:50
  266.2 182.3 %all-gather.13.cloned.1.call-start = ((), (), s32[]{:S(2)}) async-start(), calls=%async_computation.10 | async-start | bytes 5898240 | tf_op jit(solution)/shard_map/all_gather | solution.py:51
  266.7 269.6 %all-gather.17.cloned.1.call-start = ((), (), s32[]{:S(2)}) async-start(), calls=%async_computation.12 | async-start | bytes 3932160 | tf_op jit(solution)/shard_map/all_gather | solution.py:134
  295.8 62.8 %copy-start.1 = (bf16[512,768]{1,0:T(8,128)(2,1)S(1)}, bf16[512,768]{1,0:T(8,128)(2,1)}, u32[]{:S(2)}) copy-start(bf16[512,768]{1,0:T(8,128)(2,1)} %param.13) | copy-start | bytes 2359300
  328.8 119.7 %copy-start.29 = (f32[768]{0:T(1024)S(1)}, f32[768]{0:T(1024)}, u32[]{:S(2)}) copy-start(f32[768]{0:T(1024)} %param.18) | copy-start | bytes 9220
  361.6 99.6 %copy-start.7 = (f32[512,768]{1,0:T(8,128)}, f32[512,768]{1,0:T(8,128)S(1)}, u32[]{:S(2)}) copy-start(f32[512,768]{1,0:T(8,128)S(1)} %get-tuple-element.334) | copy-start | bytes 4718596
  361.6 99.6 %copy-start.22 = (f32[512]{0:T(512)}, f32[512]{0:T(512)S(1)}, u32[]{:S(2)}) copy-start(f32[512]{0:T(512)S(1)} %broadcast_multiply_fusion) | copy-start | bytes 6148
  361.9 99.3 %copy-start.25 = (f32[512]{0:T(512)}, f32[512]{0:T(512)S(1)}, u32[]{:S(2)}) copy-start(f32[512]{0:T(512)S(1)} %fusion.73) | copy-start | bytes 6148
  473.7 333.8 %reduce-scatter.9.cloned.1.call-start = ((), (), s32[]{:S(2)}) async-start(), calls=%async_computation.13 | async-start | bytes 3932160 | tf_op jit(solution)/shard_map/reduce_scatter | solution.py:168
  554.0 10.1 copy-start.4
  602.4 10.1 copy-start.4
  651.9 10.1 copy-start.4
  701.3 10.1 copy-start.4
  748.5 91.2 %reduce-scatter.13.cloned.1.call-start = ((), (), s32[]{:S(2)}) async-start(), calls=%async_computation.15 | async-start | bytes 1474560 | tf_op jit(solution)/shard_map/reduce_scatter | solution.py:190
  751.8 174.0 %reduce-scatter.15.cloned.1.call-start = ((), (), s32[]{:S(2)}) async-start(), calls=%async_computation.16 | async-start | bytes 5898240 | tf_op jit(solution)/shard_map/reduce_scatter | solution.py:196
  759.2 254.7 %reduce-scatter.17.cloned.1.call-start = ((), (), s32[]{:S(2)}) async-start(), calls=%async_computation.17 | async-start | bytes 5898240 | tf_op jit(solution)/shard_map/reduce_scatter | solution.py:199
  768.7 314.9 %reduce-scatter.11.cloned.1.call-start = ((), (), s32[]{:S(2)}) async-start(), calls=%async_computation.14 | async-start | bytes 4423680 | tf_op jit(solution)/shard_map/reduce_scatter | solution.py:187
  768.9 38.6 %copy-start.2 = (bf16[512,768]{1,0:T(8,128)(2,1)S(1)}, bf16[512,768]{1,0:T(8,128)(2,1)}, u32[]{:S(2)}) copy-start(bf16[512,768]{1,0:T(8,128)(2,1)} %param.13) | copy-start | bytes 2359300
  768.9 38.6 %copy-start.14 = (f32[512]{0:T(512)S(1)}, f32[512]{0:T(512)}, u32[]{:S(2)}) copy-start(f32[512]{0:T(512)} %copy-done.13) | copy-start | bytes 6148
  768.9 38.6 %copy-start.16 = (f32[512]{0:T(512)S(1)}, f32[512]{0:T(512)}, u32[]{:S(2)}) copy-start(f32[512]{0:T(512)} %copy-done.15) | copy-start | bytes 6148
  768.9 38.6 %copy-start.21 = (f32[768]{0:T(1024)S(1)}, f32[768]{0:T(1024)}, u32[]{:S(2)}) copy-start(f32[768]{0:T(1024)} %param.15) | copy-start | bytes 9220
  770.1 37.5 %copy-start.10 = (bf16[512,768]{1,0:T(8,128)(2,1)S(1)}, bf16[512,768]{1,0:T(8,128)(2,1)}, u32[]{:S(2)}) copy-start(bf16[512,768]{1,0:T(8,128)(2,1)} %copy.73) | copy-start | bytes 2359300
  814.7 204.1 %copy-start.20 = (f32[512]{0:T(512)S(1)}, f32[512]{0:T(512)}, u32[]{:S(2)}) copy-start(f32[512]{0:T(512)} %copy-done.19) | copy-start | bytes 6148
  814.7 208.0 %copy-start.24 = (bf16[768]{0:T(1024)(128)(2,1)S(1)}, bf16[768]{0:T(1024)(128)(2,1)}, u32[]{:S(2)}) copy-start(bf16[768]{0:T(1024)(128)(2,1)} %get-tuple-element.273) | copy-start | bytes 4612
  814.7 220.8 %copy-start.18 = (f32[512]{0:T(512)S(1)}, f32[512]{0:T(512)}, u32[]{:S(2)}) copy-start(f32[512]{0:T(512)} %copy-done.17) | copy-start | bytes 6148
  1035.6 48.0 %copy-start.12 = (bf16[192,768]{1,0:T(8,128)(2,1)S(1)}, bf16[192,768]{1,0:T(8,128)(2,1)}, u32[]{:S(2)}) copy-start(bf16[192,768]{1,0:T(8,128)(2,1)} %reduce-scatter.13.cloned.1.call-done) | copy-start | bytes 884740
  (21 other events, 73.4 us)
Sparse Core Ops, SparseCore 0:
  9.6 72.6 all-gather.6
  87.9 62.0 all-gather.8
  151.6 88.0 all-gather.14
  265.7 60.8 reduce-scatter.6
  328.0 30.4 all-gather.10
  359.9 88.5 all-gather.12
  473.8 62.4 all-gather.16
  748.6 58.8 reduce-scatter.8
  810.4 29.1 reduce-scatter.12
  841.8 83.9 reduce-scatter.14
  928.1 85.7 reduce-scatter.16
  1016.1 67.4 reduce-scatter.10
where the time goes:
time: 1240 us
  waiting for transfers between devices  602 us (49%)
  matrix products  300 us (24%)
  blocking collectives  191 us (15%)
  local copies, waits for them, and re-layouts  78.1 us (6%)
  other arithmetic  41.1 us (3%)
  between operations  17.3 us (1%)
    psum x1, blocking collectives, body(): lax.psum((lax.psum_scatter(d_gain_attn.astype(jnp.bfloat16), 'ka', scatte...  145 us
    reduce_scatter x1, waiting for transfers between devices, body(): lax.psum_scatter(d_w_down.astype(jnp.bfloat16), 'ka', scatter_dimension=0...  88.1 us
    all_gather x1, waiting for transfers between devices, body(): lax.all_gather(w_up, 'ka', axis=0, tiled=True)  86.6 us
    reduce_scatter x1, waiting for transfers between devices, body(): lax.psum_scatter(d_w_up.astype(jnp.bfloat16), 'ka', scatter_dimension=0,...  86.2 us
    all_gather x1, waiting for transfers between devices, body(): lax.all_gather(w_qkv, 'ka', axis=0, tiled=True)  70.9 us
    dot_general x4, matrix products, backward_block(): jnp.einsum('qhd,khd->hqk', grad_blk, values_own, preferred_element_type=j...  67.3 us
    all_gather x1, waiting for transfers between devices, body(): queries_all = lax.all_gather(projected[:, :D], 'ka', axis=0, tiled=True)  58.9 us
    dot_general x4, matrix products, backward_block(): jnp.einsum('hqk,qhd->khd', signed, grad_blk, preferred_element_type=jnp.f...  53.5 us
  transfers between devices with their start and end apart: 12, of which 11 were waited for; matrix products, arithmetic and copies ran while one was open for 14% of the time, Pallas kernels for 0%

commit v1 on v0

--- a/solution.py
+++ b/solution.py
@@ -1,13 +1,442 @@
+import functools
 import math
 
 import jax
 import jax.numpy as jnp
 from jax import lax
+from jax.experimental import pallas as pl
+from jax.experimental.pallas import tpu as pltpu
 from jax.sharding import PartitionSpec as P
 
 D = 768
 HEADS = 12
 HEAD = 64
+SPAN = 4
+LOCAL = HEADS // SPAN
+WIDE = LOCAL * HEAD
+LOG2E = 1.4426950408889634
+MESH = pl.DeviceIdType.MESH
+BF = jnp.bfloat16
+F32 = jnp.float32
+
+
+def mirror(depth, side):
+    return depth + side * (SPAN - 1 - 2 * depth)
+
+
+def neighbours(pb):
+    across_x = pb + 2 - 4 * ((pb // 2) % 2)
+    across_y = pb + 4 - 8 * ((pb // 4) % 2)
+    across_both = across_x + 4 - 8 * ((across_x // 4) % 2)
+    return across_x, across_y, across_both
+
+
+def sibling_of(pb):
+    return pb + 1 - 2 * (pb % 2)
+
+
+def far(src, dst, send_sem, recv_sem, pb, ka):
+    return pltpu.make_async_remote_copy(
+        src, dst, send_sem, recv_sem, device_id=(pb, ka), device_id_type=MESH
+    )
+
+
+def greet(peers):
+    barrier = pltpu.get_barrier_semaphore()
+    for peer in peers:
+        pl.semaphore_signal(barrier, 1, device_id=peer, device_id_type=MESH)
+    pl.semaphore_wait(barrier, len(peers))
+
+
+def dot_nt(left, right):
+    return lax.dot_general(left, right, (((1,), (1,)), ((), ())), preferred_element_type=F32)
+
+
+def dot_tn(left, right):
+    return lax.dot_general(left, right, (((0,), (0,)), ((), ())), preferred_element_type=F32)
+
+
+def dot_nn(left, right):
+    return jnp.dot(left, right, preferred_element_type=F32)
+
+
+def fold_lanes(tile):
+    out = tile[:, :128]
+    for at in range(128, tile.shape[1], 128):
+        out = out + tile[:, at : at + 128]
+    return out
+
+
+def forward_kernel(
+    xa, wq4, start, wo, wu, wd,
+    ohome, xg_out, wq_out, q_out, k_out, v_out, ah_out, tot_out, start_out, wog, wug, wdg,
+    xg, wqs, qs, ks, vs, ahs, tots, ob, starts,
+    send_x, recv_x, send_q, recv_q, send_s, recv_s, send_o, recv_o,
+    send_z, recv_z, send_p, recv_p, send_c, recv_c, own_sem, out_sem,
+):
+    pb = lax.axis_index("pb")
+    ka = lax.axis_index("ka")
+    core = pb % 2
+    base = pb - core
+    side = ka // 2
+    depth = mirror(ka, side)
+    home_u = mirror(ka, core)
+    quarter = 2 * depth + core
+    sibling = sibling_of(pb)
+    plane = neighbours(pb)
+    rows = xa.shape[0]
+    half = rows // 2
+    rank = (pb // 2) % 4
+
+    column = [((base + k), (ka + i) % SPAN) for i in range(SPAN) for k in range(2)]
+    greet(
+        [(pb, (ka + i) % SPAN) for i in range(1, SPAN)]
+        + [(sibling, (ka + i) % SPAN) for i in range(SPAN)]
+        + [(p, ka) for p in plane]
+    )
+
+    odd = (((home_u + 1) // 2) % 2) * (1 - home_u // 2)
+    goal = mirror(1 - odd, core)
+    out_x = [
+        far(xa.at[pl.ds(h * half, half)], xg.at[ka, h], send_x.at[h], recv_x.at[ka, h], base + h, goal)
+        for h in range(2)
+    ]
+    for copy in out_x:
+        copy.start()
+
+    at_home = core == side
+
+    def near_copies():
+        remote = [
+            far(xa.at[pl.ds(h * half, half)], xg.at[ka, h], send_x.at[2 + h], recv_x.at[ka, h], sibling, ka)
+            for h in range(2)
+        ]
+        local = [
+            pltpu.make_async_copy(xa.at[pl.ds(h * half, half)], xg.at[ka, h], recv_x.at[ka, h])
+            for h in range(2)
+        ]
+        return remote, local
+
+    @pl.when(at_home)
+    def _():
+        remote, local = near_copies()
+        for copy in remote + local:
+            copy.start()
+
+    def start_copies():
+        out = []
+        for n, (d, k) in enumerate(((0, 1), (1, 0), (1, 1))):
+            target = base + (core + k) % 2
+            out.append(far(start, starts, send_s.at[n], recv_s, target, mirror(d, core)))
+        return out
+
+    @pl.when(home_u == 0)
+    def _():
+        for copy in start_copies():
+            copy.start()
+        pltpu.make_async_copy(start, starts, recv_s).start()
+
+    out_q = []
+    for i in range(1, SPAN):
+        z = (ka + i) % SPAN
+        zd = mirror(z, z // 2)
+        out_q.append(
+            far(wq4.at[2 * zd + core], wqs.at[ka], send_q.at[i - 1], recv_q.at[i - 1], pb, z)
+        )
+    for copy in out_q:
+        copy.start()
+    own_q = pltpu.make_async_copy(wq4.at[quarter], wqs.at[ka], own_sem.at[0])
+    own_q.start()
+    own_w = [
+        pltpu.make_async_copy(src, dst.at[ka], own_sem.at[1 + n])
+        for n, (src, dst) in enumerate(((wo, wog), (wu, wug), (wd, wdg)))
+    ]
+    for copy in own_w:
+        copy.start()
+
+    spread = []
+    for i in range(3):
+        u = (1 - depth) if i == 0 else i + 1
+        b = mirror(u, side)
+        far(xg.at[b, core], xg.at[b, core], send_x.at[4], recv_x.at[b, core], pb, ka).wait_recv()
+        copy = far(xg.at[b, core], xg.at[b, core], send_x.at[4 + i], recv_x.at[b, core], sibling, ka)
+        copy.start()
+        spread.append(copy)
+        if i >= 1:
+            onward = far(
+                xg.at[b, core], xg.at[b, core], send_x.at[6 + i], recv_x.at[b, core], pb, mirror(0, side)
+            )
+
+            @pl.when(depth == 1)
+            def _():
+                onward.start()
+
+            spread.append(onward)
+    b_near = ka
+    for h in range(2):
+        far(xg.at[b_near, h], xg.at[b_near, h], send_x.at[4], recv_x.at[b_near, h], pb, ka).wait_recv()
+    for i in range(3):
+        u = (1 - depth) if i == 0 else i + 1
+        b = mirror(u, side)
+        far(xg.at[b, 1 - core], xg.at[b, 1 - core], send_x.at[4], recv_x.at[b, 1 - core], pb, ka).wait_recv()
+
+    parts = (
+        (wo, wog, wo.shape[0] // 4, wo.shape[1] // 2),
+        (wu, wug, wu.shape[0] // 4, wu.shape[1] // 2),
+        (wd, wdg, wd.shape[0] // 4, wd.shape[1] // 2),
+    )
+
+    def piece(ref, n):
+        _, _, r, c = parts[n]
+        return ref.at[pl.ds(pl.multiple_of(rank * r, 16), r), pl.ds(pl.multiple_of(core * c, 128), c)]
+
+    def strip(ref, n):
+        _, _, _, c = parts[n]
+        return ref.at[:, pl.ds(pl.multiple_of(core * c, 128), c)]
+
+    def strip_other(ref, n):
+        _, _, _, c = parts[n]
+        return ref.at[:, pl.ds(pl.multiple_of((1 - core) * c, 128), c)]
+
+    along_z = []
+    for i in range(1, SPAN):
+        z = (ka + i) % SPAN
+        for n, (src, dst, _, _) in enumerate(parts):
+            along_z.append(
+                far(piece(src, n), piece(dst.at[ka], n), send_z.at[n, i - 1], recv_z.at[n, i - 1], pb, z)
+            )
+    for copy in along_z:
+        copy.start()
+
+    for i in range(1, SPAN):
+        far(wq4.at[quarter], wqs.at[(ka - i) % SPAN], send_q.at[0], recv_q.at[i - 1], pb, ka).wait_recv()
+    own_q.wait()
+    pltpu.make_async_copy(start, starts, recv_s).wait()
+
+    def project(b, carry):
+        xb = xg[b].reshape(rows, D)
+        at = pl.multiple_of(b * rows, rows)
+        for dst, col in ((qs, 0), (ks, WIDE), (vs, 2 * WIDE)):
+            w = wqs[:, :, col : col + WIDE].reshape(D, WIDE)
+            out = dot_nn(xb, w).astype(BF)
+            for h in range(LOCAL):
+                dst[h, pl.ds(at, rows), :] = out[:, h * HEAD : (h + 1) * HEAD]
+        return carry
+
+    lax.fori_loop(0, SPAN, project, 0)
+
+    in_plane = []
+
+    def begin_plane():
+        for i in range(1, SPAN):
+            z = (ka - i) % SPAN
+            for n, (src, dst, _, _) in enumerate(parts):
+                far(piece(src, n), piece(dst.at[z], n), send_z.at[n, 0], recv_z.at[n, i - 1], pb, ka).wait_recv()
+                for m, p in enumerate(plane):
+                    copy = far(
+                        piece(dst.at[z], n), piece(dst.at[z], n),
+                        send_p.at[n, i - 1, m], recv_p.at[n, i - 1, m], p, ka,
+                    )
+                    copy.start()
+                    in_plane.append(copy)
+
+    across = []
+
+    def begin_across():
+        for i in range(1, SPAN):
+            z = (ka - i) % SPAN
+            for n, (src, dst, _, _) in enumerate(parts):
+                for m in range(3):
+                    far(
+                        piece(dst.at[z], n), piece(dst.at[z], n),
+                        send_p.at[n, i - 1, m], recv_p.at[n, i - 1, m], pb, ka,
+                    ).wait_recv()
+                copy = far(
+                    strip(dst.at[z], n), strip(dst.at[z], n), send_c.at[n, i - 1], recv_c.at[n, i - 1], sibling, ka
+                )
+                copy.start()
+                across.append(copy)
+
+    scale = LOG2E / math.sqrt(HEAD)
+    one = starts[0:1, 0:1] > (SPAN // 2) * rows + 0.5
+    sub = 256
+
+    def tile_terms(q, at, width):
+        s = dot_nt(q, ks_at(at, width)) * scale
+        return jnp.exp2(s - 1.0), jnp.exp2(-s - 1.0)
+
+    def attend(h, carry):
+        def ks_at(at, width):
+            return ks[h, pl.ds(at, width), :]
+
+        def full(q, at, acc, tot):
+            s = dot_nt(q, ks[h, pl.ds(at, rows), :]) * scale
+            up, down = jnp.exp2(s - 1.0), jnp.exp2(-s - 1.0)
+            tot = tot + fold_lanes(up + down)
+            acc = acc + dot_nn((up - down).astype(BF), vs[h, pl.ds(at, rows), :])
+            return acc, tot
+
+        return carry
+
+    def attend_block(b):
+        for h in range(LOCAL):
+            for part in range(rows // sub):
+                row0 = b * rows + part * sub
+                q = qs[h, row0 : row0 + sub, :]
+
+                def full(kb, state, q=q, h=h):
+                    acc, tot = state
+                    at = pl.multiple_of(kb * rows, rows)
+                    s = dot_nt(q, ks[h, pl.ds(at, rows), :]) * scale
+                    up, down = jnp.exp2(s - 1.0), jnp.exp2(-s - 1.0)
+                    tot = tot + fold_lanes(up + down)
+                    acc = acc + dot_nn((up - down).astype(BF), vs[h, pl.ds(at, rows), :])
+                    return acc, tot
+
+                state = (jnp.zeros((sub, HEAD), F32), jnp.zeros((sub, 128), F32))
+                if b >= SPAN // 2:
+                    acc, tot = lax.fori_loop(0, SPAN // 2, full, state)
+                    state = (jnp.where(one, acc, 0.0), jnp.where(one, tot, 0.0))
+                    state = lax.fori_loop(SPAN // 2, b, full, state)
+                else:
+                    state = lax.fori_loop(0, b, full, state)
+                acc, tot = state
+                width = (part + 1) * sub
+                s = dot_nt(q, ks[h, b * rows : b * rows + width, :]) * scale
+                seen = (
+                    lax.broadcasted_iota(jnp.int32, (sub, width), 0) + part * sub
+                    >= lax.broadcasted_iota(jnp.int32, (sub, width), 1)
+                )
+                up = jnp.where(seen, jnp.exp2(s - 1.0), 0.0)
+                down = jnp.where(seen, jnp.exp2(-s - 1.0), 0.0)
+                tot = tot + fold_lanes(up + down)
+                acc = acc + dot_nn((up - down).astype(BF), vs[h, b * rows : b * rows + width, :])
+                total = jnp.sum(tot, axis=1, keepdims=True)
+                heads = acc / total
+                ahs[h, row0 : row0 + sub, :] = heads
+                tots[h, row0 : row0 + sub, :] = jnp.broadcast_to(total, (sub, HEAD))
+
+    send_back = []
+    for b in range(SPAN):
+        attend_block(b)
+        joined = jnp.concatenate(
+            [ahs[h, b * rows : (b + 1) * rows, :] for h in range(LOCAL)], axis=1
+        )
+        ob[b] = joined.astype(BF)
+        if b == 0:
+            begin_plane()
+        if b == 2:
+            begin_across()
+        remote = far(ob.at[b], ohome.at[quarter], send_o.at[b], recv_o.at[quarter], base + side, b)
+        mine = (core == side) & (ka == b)
+
+        @pl.when(jnp.logical_not(mine))
+        def _():
+            remote.start()
+
+        @pl.when(mine)
+        def _():
+            pltpu.make_async_copy(ob.at[b], ohome.at[quarter], recv_o.at[quarter]).start()
+
+        send_back.append((mine, remote))
+
+    saves = [
+        pltpu.make_async_copy(src, dst, out_sem.at[n])
+        for n, (src, dst) in enumerate(
+            (
+                (xg, xg_out), (wqs, wq_out), (qs, q_out), (ks, k_out), (vs, v_out),
+                (ahs, ah_out), (tots, tot_out), (starts, start_out),
+            )
+        )
+    ]
+    for copy in saves:
+        copy.start()
+
+    for i in range(1, SPAN):
+        z = (ka - i) % SPAN
+        for n, (src, dst, _, _) in enumerate(parts):
+            far(
+                strip_other(dst.at[z], n), strip_other(dst.at[z], n),
+                send_c.at[n, 0], recv_c.at[n, i - 1], pb, ka,
+            ).wait_recv()
+    for n in range(SPAN):
+        far(ob.at[0], ohome.at[n], send_o.at[0], recv_o.at[n], pb, ka).wait_recv()
+    for copy in saves + own_w:
+        copy.wait()
+    for copy in out_x + out_q + along_z + in_plane + across:
+        copy.wait_send()
+    for n in range(3):
+        spread[(0, 1, 3)[n]].wait_send()
+
+    @pl.when(depth == 1)
+    def _():
+        spread[2].wait_send()
+        spread[4].wait_send()
+
+    @pl.when(at_home)
+    def _():
+        remote, _ = near_copies()
+        for copy in remote:
+            copy.wait_send()
+
+    @pl.when(home_u == 0)
+    def _():
+        for copy in start_copies():
+            copy.wait_send()
+
+    for mine, remote in send_back:
+
+        @pl.when(jnp.logical_not(mine))
+        def _():
+            remote.wait_send()
+
+
+def forward_call(xa, wq4, start, wo, wu, wd):
+    rows = xa.shape[0]
+    group = rows * SPAN
+    anyspace = pl.BlockSpec(memory_space=pl.ANY)
+    vmem = pl.BlockSpec(memory_space=pltpu.VMEM)
+    shape = jax.ShapeDtypeStruct
+    dma = pltpu.SemaphoreType.DMA
+    outs = (
+        shape((SPAN, rows, WIDE), BF),
+        shape((SPAN, 2, rows // 2, D), BF),
+        shape((SPAN, D // SPAN, 3 * WIDE), BF),
+        shape((LOCAL, group, HEAD), BF),
+        shape((LOCAL, group, HEAD), BF),
+        shape((LOCAL, group, HEAD), BF),
+        shape((LOCAL, group, HEAD), F32),
+        shape((LOCAL, group, HEAD), F32),
+        shape((8, 128), F32),
+        shape((SPAN,) + wo.shape, BF),
+        shape((SPAN,) + wu.shape, BF),
+        shape((SPAN,) + wd.shape, BF),
+    )
+    vm = pltpu.VMEM
+    scratch = [
+        vm((SPAN, 2, rows // 2, D), BF),
+        vm((SPAN, D // SPAN, 3 * WIDE), BF),
+        vm((LOCAL, group, HEAD), BF),
+        vm((LOCAL, group, HEAD), BF),
+        vm((LOCAL, group, HEAD), BF),
+        vm((LOCAL, group, HEAD), F32),
+        vm((LOCAL, group, HEAD), F32),
+        vm((SPAN, rows, WIDE), BF),
+        vm((8, 128), F32),
+        dma((9,)), dma((SPAN, 2)), dma((3,)), dma((3,)), dma((3,)), dma, dma((SPAN,)), dma((SPAN,)),
+        dma((3, 3)), dma((3, 3)), dma((3, 3, 3)), dma((3, 3, 3)), dma((3, 3)), dma((3, 3)), dma((4,)), dma((8,)),
+    ]
+    return pl.pallas_call(
+        forward_kernel,
+        out_shape=outs,
+        in_specs=[vmem, anyspace, vmem, anyspace, anyspace, anyspace],
+        out_specs=(anyspace,) * len(outs),
+        scratch_shapes=scratch,
+        compiler_params=pltpu.CompilerParams(
+            collective_id=0, has_side_effects=True, vmem_limit_bytes=56 << 20
+        ),
+        name="forward_attention",
+    )(xa, wq4, start, wo, wu, wd)
 
 
 def normalize(values):
@@ -45,14 +474,15 @@
     block_count = group_rows // block_rows
     score_scale = 1.0 / math.sqrt(HEAD)
     split_at = second_start[0]
-    full_qkv, full_out, full_up, full_down = (
-        lax.all_gather(w_qkv, "ka", axis=0, tiled=True),
-        lax.all_gather(w_out, "ka", axis=0, tiled=True),
-        lax.all_gather(w_up, "ka", axis=0, tiled=True),
-        lax.all_gather(w_down, "ka", axis=0, tiled=True),
-    )
+    full_qkv = lax.all_gather(w_qkv, "ka", axis=0, tiled=True)
     inputs32 = layer_input.astype(jnp.float32)
     attn_in = (normalize(inputs32) * gain_attn).astype(jnp.bfloat16)
+    wq4 = w_qkv.reshape(D // SPAN, 3, SPAN, WIDE).transpose(2, 0, 1, 3).reshape(SPAN, D // SPAN, 3 * WIDE)
+    start = jnp.full((8, 128), split_at, F32)
+    got = forward_call(attn_in, wq4, start, w_out, w_up, w_down)
+    full_out = got[9].reshape(D, D)
+    full_up = got[10].reshape(D, -1)
+    full_down = got[11].reshape(-1, D)
     projected = jnp.dot(attn_in, full_qkv, preferred_element_type=jnp.float32).astype(jnp.bfloat16)
     keys_own = projected[:, D : 2 * D].reshape(row_count, HEADS, HEAD)
     values_own = projected[:, 2 * D :].reshape(row_count, HEADS, HEAD)
@@ -99,7 +529,7 @@
     own_sums = lax.dynamic_slice_in_dim(sums_all, kv_index * row_count, row_count, 1)
     row_totals = own_sums.T[:, :, None]
     attn_heads = own_out.reshape(row_count, HEADS, HEAD) / row_totals
-    attn_low = attn_heads.reshape(row_count, D).astype(jnp.bfloat16)
+    attn_low = got[0].transpose(1, 0, 2).reshape(row_count, D)
     attn_branch = jnp.dot(attn_low, full_out, preferred_element_type=jnp.float32)
     middle = inputs32 + attn_branch
     mlp_in = (normalize(middle) * gain_mlp).astype(jnp.bfloat16)

time: 1240 us -> 1250 us (level)
  Pallas kernels: 0 us -> 184 us
  waiting for transfers between devices: 602 us -> 428 us
    all_gather x4 -> x1, waiting for transfers between devices: 187 us -> 0.02 us  [body(): full_qkv = lax.all_gather(w_qkv, 'ka', axis=0, tiled=True)]
    pallas_call x0 -> x1, Pallas kernels: none -> 184 us  [forward_call(): pl.pallas_call(forward_kernel, out_shape=outs, in_specs=[vmem, anyspace,...]
    reduce_scatter x1, waiting for transfers between devices: 29 us -> 45.4 us  [body(): lax.psum_scatter(partial_out.astype(jnp.bfloat16), 'ka', scatter_dimensio...]
    all_gather x1, waiting for transfers between devices: 58.9 us -> 43.6 us  [body(): queries_all = lax.all_gather(projected[:, :D], 'ka', axis=0, tiled=True)]
    all_gather x1, waiting for transfers between devices: 45.4 us -> 59.8 us  [body(): lax.all_gather(d_mixed, 'ka', axis=0, tiled=True)]
  transfers between devices with their start and end apart: 12 -> 9, of which waited for: 11 -> 8; matrix products, arithmetic and copies ran while one was open for 14% -> 8% of each run, Pallas kernels for 0% -> 15%
where the time goes in v1:
time: 1250 us
  waiting for transfers between devices  428 us (34%)
  matrix products  296 us (24%)
  blocking collectives  187 us (15%)
  Pallas kernels  184 us (15%)
  local copies, waits for them, and re-layouts  87.9 us (7%)
  other arithmetic  39.2 us (3%)
  between operations  17.8 us (1%)
    pallas_call x1, Pallas kernels, forward_call(): pl.pallas_call(forward_kernel, out_shape=outs, in_specs=[vmem, anyspace,...  184 us
    psum x1, blocking collectives, body(): lax.psum((lax.psum_scatter(d_gain_attn.astype(jnp.bfloat16), 'ka', scatte...  145 us
    reduce_scatter x1, waiting for transfers between devices, body(): lax.psum_scatter(d_w_down.astype(jnp.bfloat16), 'ka', scatter_dimension=0...  88.1 us
    reduce_scatter x1, waiting for transfers between devices, body(): lax.psum_scatter(d_w_up.astype(jnp.bfloat16), 'ka', scatter_dimension=0,...  86.3 us
    dot_general x4, matrix products, backward_block(): jnp.einsum('qhd,khd->hqk', grad_blk, values_own, preferred_element_type=j...  67.3 us
    all_gather x1, waiting for transfers between devices, body(): lax.all_gather(d_mixed, 'ka', axis=0, tiled=True)  59.8 us
    dot_general x4, matrix products, backward_block(): jnp.einsum('hqk,qhd->khd', signed, grad_blk, preferred_element_type=jnp.f...  53.5 us
    dot_general x4, matrix products, forward_block(): jnp.einsum('hqk,khd->qhd', signed, values_own, preferred_element_type=jnp...  49.4 us
  transfers between devices with their start and end apart: 9, of which 8 were waited for; matrix products, arithmetic and copies ran while one was open for 8% of the time, Pallas kernels for 15%

profile of v1, /device:TPU:0, one launch (start us, length us, event | category | flops | bytes accessed | tf_op | source)
XLA Modules:
  0.0 1245.7 jit_solution(11693595856820297927)
XLA Ops:
  16.4 183.6 %forward_attention.1 = (bf16[4,512,192]{2,1,0:T(8,128)(2,1)}, bf16[4,2,256,768]{3,2,1,0:T(8,128)(2,1)}, bf16[4,192,576]{2,1,0:T(8,128)(2,1)}, bf16[3,2048,64]{2,...) custom-call(bf16[512,768]{1,0:T(8,128)(2,1)} %fusion.66.xa, ...), custom_call_target="tpu_custom_call" | custom-call | tf_op jit(solution)/shard_map/forward_attention/pallas_call | solution.py:429
  213.7 9.4 fusion.56
  226.8 5.5 multiply_reduce_fusion
  237.0 43.6 %all-gather.6.cloned.1.call-done = bf16[2048,768]{1,0:T(8,128)(2,1)} async-done(((bf16[512,768]{1,0:T(8,128)(2,1)}), bf16[2048,768]{1,0:T(8,128)(2,1)}) %all-gather.6.cloned.1.call-update) | async-done | bytes 3145744 | tf_op jit(solution)/shard_map/all_gather | solution.py:511
  294.0 100.8 %while.28 = (s32[]{:T(128)}, bf16[4,512,768]{2,1,0:T(8,128)(2,1)}, bf16[4,12,512]{2,1,0:T(8,128)(2,1)S(1)}, s32[4]{0:T(128)S(1)}, s32[]{:T(128)}, /*index=5*/bf1...) while((s32[]{:T(128)}, bf16[4,512,768]{2,1,0:T(8,128)(2,1)}, ...), condition=%wide.region_8.9_spmd.clone, body=%wide.region_6.8_spmd.clone.sunk | while | flops 893907968 | bytes 45930668 | solution.py:522
  305.7 12.4 fusion.131
  330.8 12.4 fusion.131
  355.9 12.4 fusion.131
  381.1 12.4 fusion.131
  394.9 17.1 %psum.56 = bf16[12,2048]{1,0:T(8,128)(2,1)S(1)} all-reduce(bf16[12,2048]{1,0:T(8,128)(2,1)S(1)} %bitcast.175), channel_id=1, replica_groups=mesh['pb'=8,'ka'=4] {'ka'}, use_global_device_ids=true, to_apply=%region_9.10 | all-reduce | flops 24576 | bytes 98304 | tf_op jit(solution)/shard_map/psum | solution.py:525
  419.0 59.8 %all-gather.8.cloned.1.call-done = bf16[2048,768]{1,0:T(8,128)(2,1)} async-done(((bf16[512,768]{1,0:T(8,128)(2,1)}), bf16[2048,768]{1,0:T(8,128)(2,1)}) %all-gather.8.cloned.1.call-update) | async-done | bytes 3145744 | tf_op jit(solution)/shard_map/all_gather | solution.py:564
  484.0 6.2 reshape.284
  494.5 45.4 %reduce-scatter.7.cloned.1.call-done = bf16[512,768]{1,0:T(8,128)(2,1)} async-done(((bf16[2048,768]{1,0:T(8,128)(2,1)}), bf16[512,768]{1,0:T(8,128)(2,1)}) %reduce-scatter.7.cloned.1.call-update) | async-done | bytes 786448 | tf_op jit(solution)/shard_map/reduce_scatter | solution.py:526
  544.4 13.2 %all_gather.15 = bf16[12,2048]{1,0:T(8,128)(2,1)S(1)} all-gather(bf16[12,512]{1,0:T(8,128)(2,1)S(1)} %fusion.75), channel_id=1, replica_groups=mesh['pb'=8,'ka'=4] {'ka'}, dimensions={1}, use_global_device_ids=true | all-gather | bytes 61440 | tf_op jit(solution)/shard_map/all_gather | solution.py:565
  559.5 196.5 %while.29 = (s32[]{:T(128)}, f32[512,12,64]{0,2,1:T(8,128)S(1)}, f32[512,12,64]{0,2,1:T(8,128)}, bf16[4,512,768]{2,1,0:T(8,128)(2,1)}, bf16[4,512,12,64]{1,3,2,0...) while((s32[]{:T(128)}, f32[512,12,64]{0,2,1:T(8,128)S(1)}, ...), condition=%wide.region_13.14_spmd.clone, body=%wide.region_12.13_spmd.clone.sunk | while | flops 2148666368 | bytes 137767184 | solution.py:595
  571.7 12.6 %bitcast_add_fusion.5 = f32[512,12,64]{0,2,1:T(8,128)} fusion(f32[512,12,64]{0,2,1:T(8,128)} %get-tuple-element.572, pred[]{:T(512)S(6)} %compare.3, f32[12,512,512]{2,1,0:T(8,128)S(1)} %get-tuple-element.516, pred[512,512]{1,0:T(8,128)(4,1)S(1)} %compare_and_fusion.5, u16[512,512]{1,0:T(8,128)(2,1)S(1)} %get-tuple-element.521, ...), kind=kOutput, calls=%fused_computation.46.clone.1 | convolution fusion | flops 450625536 | bytes 17301508 | tf_op jit(solution)/shard_map/while/body/eval_jaxpr/hqk,qhd->khd/dot_general | solution.py:589
  584.4 16.8 %subtract_convert_fusion.2 = bf16[12,512,512]{2,1,0:T(8,128)(2,1)S(1)} fusion(f32[12,512,512]{2,1,0:T(8,128)} %copy-done.31, f32[12,512]{1,0:T(8,128)S(1)} %bitcast.171, pred[512,512]{1,0:T(8,128)(4,1)S(1)} %compare_and_fusion.5, bf16[512,12,64]{0,2,1:T(8,128)(2,1)} %get-tuple-element.594, u16[512,512]{1,0:T(8,128)(2,1)S(1)} %get-tuple-element.521, ...), kind=kOutput, calls=%fused_computation.39.clone.1 | convolution fusion | flops 465567744 | bytes 21266436 | tf_op jit(solution)/shard_map/while/body/eval_jaxpr/qhd,khd->hqk/dot_general | solution.py:576
  620.1 13.6 %bitcast_add_fusion.5 = f32[512,12,64]{0,2,1:T(8,128)} fusion(f32[512,12,64]{0,2,1:T(8,128)} %get-tuple-element.572, pred[]{:T(512)S(6)} %compare.3, f32[12,512,512]{2,1,0:T(8,128)S(1)} %get-tuple-element.516, pred[512,512]{1,0:T(8,128)(4,1)S(1)} %compare_and_fusion.5, u16[512,512]{1,0:T(8,128)(2,1)S(1)} %get-tuple-element.521, ...), kind=kOutput, calls=%fused_computation.46.clone.1 | convolution fusion | flops 450625536 | bytes 17301508 | tf_op jit(solution)/shard_map/while/body/eval_jaxpr/hqk,qhd->khd/dot_general | solution.py:589
  633.7 16.8 %subtract_convert_fusion.2 = bf16[12,512,512]{2,1,0:T(8,128)(2,1)S(1)} fusion(f32[12,512,512]{2,1,0:T(8,128)} %copy-done.31, f32[12,512]{1,0:T(8,128)S(1)} %bitcast.171, pred[512,512]{1,0:T(8,128)(4,1)S(1)} %compare_and_fusion.5, bf16[512,12,64]{0,2,1:T(8,128)(2,1)} %get-tuple-element.594, u16[512,512]{1,0:T(8,128)(2,1)S(1)} %get-tuple-element.521, ...), kind=kOutput, calls=%fused_computation.39.clone.1 | convolution fusion | flops 465567744 | bytes 21266436 | tf_op jit(solution)/shard_map/while/body/eval_jaxpr/qhd,khd->hqk/dot_general | solution.py:576
  669.5 13.6 %bitcast_add_fusion.5 = f32[512,12,64]{0,2,1:T(8,128)} fusion(f32[512,12,64]{0,2,1:T(8,128)} %get-tuple-element.572, pred[]{:T(512)S(6)} %compare.3, f32[12,512,512]{2,1,0:T(8,128)S(1)} %get-tuple-element.516, pred[512,512]{1,0:T(8,128)(4,1)S(1)} %compare_and_fusion.5, u16[512,512]{1,0:T(8,128)(2,1)S(1)} %get-tuple-element.521, ...), kind=kOutput, calls=%fused_computation.46.clone.1 | convolution fusion | flops 450625536 | bytes 17301508 | tf_op jit(solution)/shard_map/while/body/eval_jaxpr/hqk,qhd->khd/dot_general | solution.py:589
  683.1 16.8 %subtract_convert_fusion.2 = bf16[12,512,512]{2,1,0:T(8,128)(2,1)S(1)} fusion(f32[12,512,512]{2,1,0:T(8,128)} %copy-done.31, f32[12,512]{1,0:T(8,128)S(1)} %bitcast.171, pred[512,512]{1,0:T(8,128)(4,1)S(1)} %compare_and_fusion.5, bf16[512,12,64]{0,2,1:T(8,128)(2,1)} %get-tuple-element.594, u16[512,512]{1,0:T(8,128)(2,1)S(1)} %get-tuple-element.521, ...), kind=kOutput, calls=%fused_computation.39.clone.1 | convolution fusion | flops 465567744 | bytes 21266436 | tf_op jit(solution)/shard_map/while/body/eval_jaxpr/qhd,khd->hqk/dot_general | solution.py:576
  718.9 13.6 %bitcast_add_fusion.5 = f32[512,12,64]{0,2,1:T(8,128)} fusion(f32[512,12,64]{0,2,1:T(8,128)} %get-tuple-element.572, pred[]{:T(512)S(6)} %compare.3, f32[12,512,512]{2,1,0:T(8,128)S(1)} %get-tuple-element.516, pred[512,512]{1,0:T(8,128)(4,1)S(1)} %compare_and_fusion.5, u16[512,512]{1,0:T(8,128)(2,1)S(1)} %get-tuple-element.521, ...), kind=kOutput, calls=%fused_computation.46.clone.1 | convolution fusion | flops 450625536 | bytes 17301508 | tf_op jit(solution)/shard_map/while/body/eval_jaxpr/hqk,qhd->khd/dot_general | solution.py:589
  732.5 16.8 %subtract_convert_fusion.2 = bf16[12,512,512]{2,1,0:T(8,128)(2,1)S(1)} fusion(f32[12,512,512]{2,1,0:T(8,128)} %copy-done.31, f32[12,512]{1,0:T(8,128)S(1)} %bitcast.171, pred[512,512]{1,0:T(8,128)(4,1)S(1)} %compare_and_fusion.5, bf16[512,12,64]{0,2,1:T(8,128)(2,1)} %get-tuple-element.594, u16[512,512]{1,0:T(8,128)(2,1)S(1)} %get-tuple-element.521, ...), kind=kOutput, calls=%fused_computation.39.clone.1 | convolution fusion | flops 465567744 | bytes 21266436 | tf_op jit(solution)/shard_map/while/body/eval_jaxpr/qhd,khd->hqk/dot_general | solution.py:576
  761.9 6.6 convolution_convert_fusion.1
  769.6 8.3 convolution_convert_fusion
  782.0 34.3 %reduce-scatter.9.cloned.1.call-done = bf16[512,768]{1,0:T(8,128)(2,1)} async-done(((bf16[2048,768]{1,0:T(8,128)(2,1)}), bf16[512,768]{1,0:T(8,128)(2,1)}) %reduce-scatter.9.cloned.1.call-update) | async-done | bytes 786448 | tf_op jit(solution)/shard_map/reduce_scatter | solution.py:598
  823.5 24.7 %reduce-scatter.13.cloned.1.call-done = bf16[192,768]{1,0:T(8,128)(2,1)} async-done(((bf16[768,768]{1,0:T(8,128)(2,1)}), bf16[192,768]{1,0:T(8,128)(2,1)}) %reduce-scatter.13.cloned.1.call-update) | async-done | bytes 294928 | tf_op jit(solution)/shard_map/reduce_scatter | solution.py:620
  848.2 86.3 %reduce-scatter.15.cloned.1.call-done = bf16[192,3072]{1,0:T(8,128)(2,1)} async-done(((bf16[768,3072]{1,0:T(8,128)(2,1)}), bf16[192,3072]{1,0:T(8,128)(2,1)}) %reduce-scatter.15.cloned.1.call-update) | async-done | bytes 1179664 | tf_op jit(solution)/shard_map/reduce_scatter | solution.py:626
  934.6 88.1 %reduce-scatter.17.cloned.1.call-done = bf16[768,768]{1,0:T(8,128)(2,1)} async-done(((bf16[3072,768]{1,0:T(8,128)(2,1)}), bf16[768,768]{1,0:T(8,128)(2,1)}) %reduce-scatter.17.cloned.1.call-update) | async-done | bytes 1179664 | tf_op jit(solution)/shard_map/reduce_scatter | solution.py:629
  1031.6 11.5 all-reduce.4
  1047.8 44.6 %reduce-scatter.11.cloned.1.call-done = bf16[192,2304]{1,0:T(8,128)(2,1)} async-done(((bf16[768,2304]{1,0:T(8,128)(2,1)}), bf16[192,2304]{1,0:T(8,128)(2,1)}) %reduce-scatter.11.cloned.1.call-update) | async-done | bytes 884752 | tf_op jit(solution)/shard_map/reduce_scatter | solution.py:617
  1092.4 144.7 %all-reduce.6 = (f32[192]{0:T(256)}, f32[192,2304]{1,0:T(8,128)}, f32[192,768]{1,0:T(8,128)}, f32[192]{0:T(256)}, f32[192,3072]{1,0:T(8,128)}, /*index=5*/f32[768,768]{1,0:T(8,128)}, f32[1]{0:T(128)}) all-reduce(f32[192]{0:T(256)S(1)} %get-tuple-element.369, ...), channel_id=1, replica_groups=mesh['pb'=8,'ka'=4] {'pb'}, use_global_device_ids=true, to_apply=%region_19.20 | all-reduce | flops 1769857 | bytes 10619910 | tf_op jit(solution)/shard_map/psum | solution.py:612
  (249 shorter events, 218.6 us)
Async XLA Ops:
  7.2 196.3 %all-gather.4.cloned.1.call-start = ((), (), s32[]{:S(2)}) async-start(), calls=%async_computation.6 | async-start | bytes 4423680 | tf_op jit(solution)/shard_map/all_gather | solution.py:477
  7.9 272.8 %all-gather.6.cloned.1.call-start = ((), (), s32[]{:S(2)}) async-start(), calls=%async_computation.7 | async-start | bytes 3932160 | tf_op jit(solution)/shard_map/all_gather | solution.py:511
  14.2 185.8 %copy-start.12 = (f32[512]{0:T(512)}, f32[512]{0:T(512)S(1)}, u32[]{:S(2)}) copy-start(f32[512]{0:T(512)S(1)} %broadcast_multiply_fusion.1) | copy-start | bytes 6148
  14.5 185.4 %copy-start.20 = (f32[512]{0:T(512)}, f32[512]{0:T(512)S(1)}, u32[]{:S(2)}) copy-start(f32[512]{0:T(512)S(1)} %fusion.68) | copy-start | bytes 6148
  14.6 185.4 %copy-start.16 = (f32[512]{0:T(512)}, f32[512]{0:T(512)S(1)}, u32[]{:S(2)}) copy-start(f32[512]{0:T(512)S(1)} %fusion.76) | copy-start | bytes 6148
  203.2 23.5 %copy-start.8 = (f32[512,768]{1,0:T(8,128)}, f32[512,768]{1,0:T(8,128)S(1)}, u32[]{:S(2)}) copy-start(f32[512,768]{1,0:T(8,128)S(1)} %get-tuple-element.342) | copy-start | bytes 4718596
  203.2 23.6 %copy-start.22 = (f32[512]{0:T(512)}, f32[512]{0:T(512)S(1)}, u32[]{:S(2)}) copy-start(f32[512]{0:T(512)S(1)} %broadcast_multiply_fusion) | copy-start | bytes 6148
  203.5 23.3 %copy-start.25 = (f32[512]{0:T(512)}, f32[512]{0:T(512)S(1)}, u32[]{:S(2)}) copy-start(f32[512]{0:T(512)S(1)} %fusion.77) | copy-start | bytes 6148
  208.8 270.0 %all-gather.8.cloned.1.call-start = ((), (), s32[]{:S(2)}) async-start(), calls=%async_computation.8 | async-start | bytes 3932160 | tf_op jit(solution)/shard_map/all_gather | solution.py:564
  208.9 14.3 %slice-start.2 = ((s8[4718592]{0:T(1024)(128)(4,1)}), s8[4194304]{0:T(1024)(128)(4,1)S(1)}, s32[]{:S(2)}) async-start(s8[4718592]{0:T(1024)(128)(4,1)} %bitcast.182), calls=%async_computation.17 | async-start | bytes 8388608
  208.9 17.9 %slice-start = ((s8[4718592]{0:T(1024)(128)(4,1)}), s8[4194304]{0:T(1024)(128)(4,1)S(1)}, s32[]{:S(2)}) async-start(s8[4718592]{0:T(1024)(128)(4,1)} %bitcast.178), calls=%async_computation.15 | async-start | bytes 8388608
  213.7 13.0 %copy-start.30 = (f32[512,3072]{1,0:T(8,128)}, f32[512,3072]{1,0:T(8,128)S(1)}, u32[]{:S(2)}) copy-start(f32[512,3072]{1,0:T(8,128)S(1)} %fusion.83) | copy-start | bytes 18874372
  213.7 13.0 %slice-start.1 = ((s8[4718592]{0:T(1024)(128)(4,1)}), s8[524288]{0:T(1024)(128)(4,1)S(1)}, s32[]{:S(2)}) async-start(s8[4718592]{0:T(1024)(128)(4,1)} %bitcast.178), calls=%async_computation.16 | async-start | bytes 1048576
  416.5 123.4 %reduce-scatter.7.cloned.1.call-start = ((), (), s32[]{:S(2)}) async-start(), calls=%async_computation.9 | async-start | bytes 3932160 | tf_op jit(solution)/shard_map/reduce_scatter | solution.py:526
  417.1 399.2 %reduce-scatter.9.cloned.1.call-start = ((), (), s32[]{:S(2)}) async-start(), calls=%async_computation.10 | async-start | bytes 3932160 | tf_op jit(solution)/shard_map/reduce_scatter | solution.py:598
  561.7 10.0 copy-start.5
  610.1 10.0 copy-start.5
  708.9 10.0 copy-start.5
  756.0 92.2 %reduce-scatter.13.cloned.1.call-start = ((), (), s32[]{:S(2)}) async-start(), calls=%async_computation.12 | async-start | bytes 1474560 | tf_op jit(solution)/shard_map/reduce_scatter | solution.py:620
  761.8 172.8 %reduce-scatter.15.cloned.1.call-start = ((), (), s32[]{:S(2)}) async-start(), calls=%async_computation.13 | async-start | bytes 5898240 | tf_op jit(solution)/shard_map/reduce_scatter | solution.py:626
  768.5 254.2 %reduce-scatter.17.cloned.1.call-start = ((), (), s32[]{:S(2)}) async-start(), calls=%async_computation.14 | async-start | bytes 5898240 | tf_op jit(solution)/shard_map/reduce_scatter | solution.py:629
  777.9 314.5 %reduce-scatter.11.cloned.1.call-start = ((), (), s32[]{:S(2)}) async-start(), calls=%async_computation.11 | async-start | bytes 4423680 | tf_op jit(solution)/shard_map/reduce_scatter | solution.py:617
  778.1 38.2 %copy-start.4 = (bf16[512,768]{1,0:T(8,128)(2,1)S(1)}, bf16[512,768]{1,0:T(8,128)(2,1)}, u32[]{:S(2)}) copy-start(bf16[512,768]{1,0:T(8,128)(2,1)} %fusion.66.xa) | copy-start | bytes 2359300
  779.3 37.0 %copy-start.10 = (bf16[512,768]{1,0:T(8,128)(2,1)S(1)}, bf16[512,768]{1,0:T(8,128)(2,1)}, u32[]{:S(2)}) copy-start(bf16[512,768]{1,0:T(8,128)(2,1)} %copy.92) | copy-start | bytes 2359300
  821.5 201.2 %copy-start.1 = (bf16[512,768]{1,0:T(8,128)(2,1)S(1)}, bf16[512,768]{1,0:T(8,128)(2,1)}, u32[]{:S(2)}) copy-start(bf16[512,768]{1,0:T(8,128)(2,1)} %param.13) | copy-start | bytes 2359300
  821.5 201.2 %copy-start.13 = (f32[512]{0:T(512)S(1)}, f32[512]{0:T(512)}, u32[]{:S(2)}) copy-start(f32[512]{0:T(512)} %copy-done.12) | copy-start | bytes 6148
  821.5 201.2 %copy-start.15 = (f32[768]{0:T(1024)S(1)}, f32[768]{0:T(1024)}, u32[]{:S(2)}) copy-start(f32[768]{0:T(1024)} %param.15) | copy-start | bytes 9220
  823.5 204.1 %copy-start.21 = (f32[512]{0:T(512)S(1)}, f32[512]{0:T(512)}, u32[]{:S(2)}) copy-start(f32[512]{0:T(512)} %copy-done.20) | copy-start | bytes 6148
  823.5 204.1 %copy-start.17 = (f32[512]{0:T(512)S(1)}, f32[512]{0:T(512)}, u32[]{:S(2)}) copy-start(f32[512]{0:T(512)} %copy-done.16) | copy-start | bytes 6148
  823.5 208.1 %copy-start.24 = (bf16[768]{0:T(1024)(128)(2,1)S(1)}, bf16[768]{0:T(1024)(128)(2,1)}, u32[]{:S(2)}) copy-start(bf16[768]{0:T(1024)(128)(2,1)} %get-tuple-element.281) | copy-start | bytes 4612
  823.5 221.0 %copy-start.19 = (f32[512]{0:T(512)S(1)}, f32[512]{0:T(512)}, u32[]{:S(2)}) copy-start(f32[512]{0:T(512)} %copy-done.18) | copy-start | bytes 6148
  1044.5 47.9 %copy-start.11 = (bf16[192,768]{1,0:T(8,128)(2,1)S(1)}, bf16[192,768]{1,0:T(8,128)(2,1)}, u32[]{:S(2)}) copy-start(bf16[192,768]{1,0:T(8,128)(2,1)} %reduce-scatter.13.cloned.1.call-done) | copy-start | bytes 884740
  (20 other events, 90.9 us)
Sparse Core Ops, SparseCore 0:
  9.6 116.3 all-gather.3
  208.9 71.6 all-gather.5
  416.6 62.1 all-gather.7
  481.0 58.8 reduce-scatter.6
  756.1 60.1 reduce-scatter.8
  819.0 29.1 reduce-scatter.12
  850.5 83.9 reduce-scatter.14
  936.9 85.7 reduce-scatter.16
  1025.0 67.3 reduce-scatter.10

commit v2 on v1

--- a/solution.py
+++ b/solution.py
@@ -88,7 +88,6 @@
     half = rows // 2
     rank = (pb // 2) % 4
 
-    column = [((base + k), (ka + i) % SPAN) for i in range(SPAN) for k in range(2)]
     greet(
         [(pb, (ka + i) % SPAN) for i in range(1, SPAN)]
         + [(sibling, (ka + i) % SPAN) for i in range(SPAN)]
@@ -260,23 +259,6 @@
     scale = LOG2E / math.sqrt(HEAD)
     one = starts[0:1, 0:1] > (SPAN // 2) * rows + 0.5
     sub = 256
-
-    def tile_terms(q, at, width):
-        s = dot_nt(q, ks_at(at, width)) * scale
-        return jnp.exp2(s - 1.0), jnp.exp2(-s - 1.0)
-
-    def attend(h, carry):
-        def ks_at(at, width):
-            return ks[h, pl.ds(at, width), :]
-
-        def full(q, at, acc, tot):
-            s = dot_nt(q, ks[h, pl.ds(at, rows), :]) * scale
-            up, down = jnp.exp2(s - 1.0), jnp.exp2(-s - 1.0)
-            tot = tot + fold_lanes(up + down)
-            acc = acc + dot_nn((up - down).astype(BF), vs[h, pl.ds(at, rows), :])
-            return acc, tot
-
-        return carry
 
     def attend_block(b):
         for h in range(LOCAL):
@@ -439,230 +421,534 @@
     )(xa, wq4, start, wo, wu, wd)
 
 
+def backward_kernel(
+    dah, xg_in, wq_in, q_in, k_in, v_in, ah_in, tot_in, starts,
+    dxh, gq,
+    da, xg, wqs, qs, ks, vs, ahs, tots, dms, deltas, dqs, dp, own, mate, back,
+    send_a, recv_a, send_m, recv_m, send_h, recv_h, in_sem,
+):
+    pb = lax.axis_index("pb")
+    ka = lax.axis_index("ka")
+    core = pb % 2
+    base = pb - core
+    side = ka // 2
+    depth = mirror(ka, side)
+    quarter = 2 * depth + core
+    sibling = sibling_of(pb)
+    rows = dah.shape[1]
+    half = rows // 2
+
+    greet(
+        [(pb, (ka + i) % SPAN) for i in range(1, SPAN)]
+        + [(sibling, (ka + i) % SPAN) for i in range(SPAN)]
+    )
+    loads = [
+        pltpu.make_async_copy(src, dst, in_sem.at[n])
+        for n, (src, dst) in enumerate(
+            (
+                (q_in, qs), (k_in, ks), (v_in, vs), (ah_in, ahs), (tot_in, tots), (xg_in, xg), (wq_in, wqs),
+            )
+        )
+    ]
+    for copy in loads:
+        copy.start()
+
+    def outgoing(n):
+        worker_depth, worker_core = n // 2, n % 2
+        target, where = base + worker_core, mirror(worker_depth, core)
+        mine = (target == pb) & (where == ka)
+        return mine, far(dah.at[n], da.at[ka], send_a.at[n], recv_a.at[ka], target, where)
+
+    for n in range(SPAN):
+        mine, remote = outgoing(n)
+
+        @pl.when(jnp.logical_not(mine))
+        def _():
+            remote.start()
+
+        @pl.when(mine)
+        def _():
+            pltpu.make_async_copy(dah.at[n], da.at[ka], recv_a.at[ka]).start()
+
+    for copy in loads[:5]:
+        copy.wait()
+    for b in range(SPAN):
+        far(dah.at[0], da.at[b], send_a.at[0], recv_a.at[b], pb, ka).wait_recv()
+
+    scale = LOG2E / math.sqrt(HEAD)
+    unit = 1.0 / math.sqrt(HEAD)
+    one = jnp.where(starts[0:1, 0:1] > (SPAN // 2) * rows + 0.5, 1.0, 0.0)
+    sub = 256
+
+    for b in range(SPAN):
+        block = da[b].astype(F32)
+        for h in range(LOCAL):
+            rows_b = slice(b * rows, (b + 1) * rows)
+            scaled = block[:, h * HEAD : (h + 1) * HEAD] / tots[h, rows_b, :]
+            dms[h, rows_b, :] = scaled.astype(BF)
+            deltas[h, :, rows_b] = lax.dot_general(
+                jnp.ones((8, HEAD), F32), scaled * ahs[h, rows_b, :],
+                (((1,), (1,)), ((), ())), precision=lax.Precision.HIGHEST, preferred_element_type=F32,
+            )
+
+    def per_head(h, carry):
+        dqs[...] = jnp.zeros_like(dqs)
+
+        def per_block(kb, carry):
+            for part in range(rows // sub):
+                at = pl.multiple_of(kb * rows + part * sub, sub)
+                keys = ks[h, pl.ds(at, sub), :]
+                values = vs[h, pl.ds(at, sub), :]
+
+                def terms(row0, width):
+                    q = qs[h, pl.ds(row0, width), :]
+                    dm = dms[h, pl.ds(row0, width), :]
+                    s = dot_nt(keys, q) * scale
+                    up, down = jnp.exp2(s - 1.0), jnp.exp2(-s - 1.0)
+                    dsig = dot_nt(values, dm)
+                    delta = deltas[h, 0:1, pl.ds(row0, width)]
+                    return q, dm, up, down, dsig, delta
+
+                def use(q, dm, expo, sine, dsig, delta):
+                    ds = (expo * dsig - sine * delta).astype(BF)
+                    return dot_nn(ds, q), dot_nn(sine.astype(BF), dm), dot_tn(ds, keys)
+
+                width = rows - part * sub
+                q, dm, up, down, dsig, delta = terms(at, width)
+                seen = lax.broadcasted_iota(jnp.int32, (sub, width), 0) <= lax.broadcasted_iota(
+                    jnp.int32, (sub, width), 1
+                )
+                up = jnp.where(seen, up, 0.0)
+                down = jnp.where(seen, down, 0.0)
+                dk, dv, dq = use(q, dm, up + down, up - down, dsig, delta)
+                dqs[pl.ds(at, width), :] += dq
+
+                def later(qb, state):
+                    dk, dv = state
+                    row0 = pl.multiple_of(qb * rows, rows)
+                    q, dm, up, down, dsig, delta = terms(row0, rows)
+                    dk1, dv1, dq1 = use(q, dm, up + down, up - down, dsig, delta)
+                    same = jnp.where(qb // 2 == kb // 2, 1.0, 0.0)
+                    keep = jnp.maximum(one, same) > 0.5
+                    dqs[pl.ds(row0, rows), :] += jnp.where(keep, dq1, 0.0)
+                    return dk + jnp.where(keep, dk1, 0.0), dv + jnp.where(keep, dv1, 0.0)
+
+                dk, dv = lax.fori_loop(kb + 1, SPAN, later, (dk, dv))
+                ks_out = pl.ds(at, sub)
+                dp[1, h, ks_out, :] = (dk * unit).astype(BF)
+                dp[2, h, ks_out, :] = dv.astype(BF)
+            return carry
+
+        lax.fori_loop(0, SPAN, per_block, 0)
+        dp[0, h] = (dqs[...] * unit).astype(BF)
+        return carry
+
+    lax.fori_loop(0, LOCAL, per_head, 0)
+
+    loads[5].wait()
+    loads[6].wait()
+    weight = wqs[...].reshape(D, 3 * WIDE)
+    total = jnp.zeros((D, 3 * WIDE), F32)
+
+    def joined(b):
+        rows_b = slice(b * rows, (b + 1) * rows)
+        return jnp.concatenate(
+            [dp[part, h, rows_b, :] for part in range(3) for h in range(LOCAL)], axis=1
+        )
+
+    def home_copy(b, d):
+        return far(back.at[b], dxh.at[depth, core], send_h.at[b], recv_h.at[depth, core], base + side, b)
+
+    swaps = []
+    for b in range(SPAN):
+        part = dot_nt(joined(b), weight)
+        own[b] = part.astype(BF).reshape(2, half, D)
+        copy = far(own.at[b, 1 - core], mate.at[b], send_m.at[b], recv_m.at[b], sibling, ka)
+        copy.start()
+        swaps.append(copy)
+    grad = dot_tn(xg[0].reshape(rows, D), joined(0))
+    for b in range(1, SPAN):
+        grad = grad + dot_tn(xg[b].reshape(rows, D), joined(b))
+    gq[...] = grad.astype(BF).reshape(gq.shape)
+    for b in range(SPAN):
+        far(own.at[b, 0], mate.at[b], send_m.at[b], recv_m.at[b], sibling, ka).wait_recv()
+        back[b] = (own[b, core].astype(F32) + mate[b].astype(F32)).astype(BF)
+        mine = (core == side) & (ka == b)
+        remote = home_copy(b, depth)
+
+        @pl.when(jnp.logical_not(mine))
+        def _():
+            remote.start()
+
+        @pl.when(mine)
+        def _():
+            pltpu.make_async_copy(back.at[b], dxh.at[depth, core], recv_h.at[depth, core]).start()
+
+    for d in range(2):
+        for k in range(2):
+            far(back.at[0], dxh.at[d, k], send_h.at[0], recv_h.at[d, k], pb, ka).wait_recv()
+    for copy in swaps:
+        copy.wait_send()
+    for n in range(SPAN):
+        mine, remote = outgoing(n)
+
+        @pl.when(jnp.logical_not(mine))
+        def _():
+            remote.wait_send()
+
+        mine_b = (core == side) & (ka == n)
+        remote_b = home_copy(n, depth)
+
+        @pl.when(jnp.logical_not(mine_b))
+        def _():
+            remote_b.wait_send()
+
+
+def backward_call(dah, xg, wq, q, k, v, ah, tot, starts):
+    rows = dah.shape[1]
+    group = rows * SPAN
+    anyspace = pl.BlockSpec(memory_space=pl.ANY)
+    vmem = pl.BlockSpec(memory_space=pltpu.VMEM)
+    shape = jax.ShapeDtypeStruct
+    dma = pltpu.SemaphoreType.DMA
+    vm = pltpu.VMEM
+    scratch = [
+        vm((SPAN, rows, WIDE), BF),
+        vm(xg.shape, BF),
+        vm(wq.shape, BF),
+        vm(q.shape, BF),
+        vm(q.shape, BF),
+        vm(q.shape, BF),
+        vm(q.shape, F32),
+        vm(q.shape, F32),
+        vm(q.shape, BF),
+        vm((LOCAL, 8, group), F32),
+        vm((group, HEAD), F32),
+        vm((3, LOCAL, group, HEAD), BF),
+        vm((SPAN, 2, rows // 2, D), BF),
+        vm((SPAN, rows // 2, D), BF),
+        vm((SPAN, rows // 2, D), BF),
+        dma((SPAN,)), dma((SPAN,)), dma((SPAN,)), dma((SPAN,)), dma((SPAN,)), dma((2, 2)), dma((7,)),
+    ]
+    return pl.pallas_call(
+        backward_kernel,
+        out_shape=(
+            shape((2, 2, rows // 2, D), BF),
+            shape((SPAN, D // SPAN, 3 * WIDE), BF),
+        ),
+        in_specs=[anyspace] * 8 + [vmem],
+        out_specs=(anyspace, vmem),
+        scratch_shapes=scratch,
+        compiler_params=pltpu.CompilerParams(
+            collective_id=1, has_side_effects=True, vmem_limit_bytes=56 << 20
+        ),
+        name="backward_attention",
+    )(dah, xg, wq, q, k, v, ah, tot, starts)
+
+
+def reduce_kernel(outer, count, *refs):
+    ins, gq = refs[:count], refs[count]
+    refs = refs[count + 1 :]
+    outs, out_q = refs[:count], refs[count]
+    refs = refs[count + 1 :]
+    halves, mates, fours, sums, zs, fins, slots = (refs[i * count : (i + 1) * count] for i in range(7))
+    refs = refs[7 * count :]
+    fours_q, sum_q, zq, fin_q, slots_q = refs[:5]
+    (
+        own_sem, send_m, recv_m, send_p, recv_p, send_z, recv_z, send_o, recv_o,
+        send_g, recv_g, send_c, recv_c, keep_sem,
+    ) = refs[5:]
+    pb = lax.axis_index("pb")
+    ka = lax.axis_index("ka")
+    core = pb % 2
+    sibling = sibling_of(pb)
+    plane = neighbours(pb)
+    rank = (pb // 2) % 4
+    where = pb // 8
+    beyond = [(pb + 8 * o) % (8 * outer) for o in range(1, outer)]
+    greet(
+        [(pb, (ka + i) % SPAN) for i in range(1, SPAN)]
+        + [(sibling, ka)]
+        + [(p, ka) for p in plane]
+        + [(p, ka) for p in beyond]
+    )
+
+    def columns(ref, k):
+        width = ref.shape[-1] // 2
+        return pl.ds(pl.multiple_of(k * width, 128), width)
+
+    def quarter(ref, r):
+        height = ref.shape[-2] // 4
+        return pl.ds(pl.multiple_of(r * height, 16), height)
+
+    started = []
+
+    def begin(copy):
+        copy.start()
+        started.append(copy)
+        return copy
+
+    local = []
+    for n in range(count):
+        src = ins[n]
+        copy = pltpu.make_async_copy(src.at[:, :, columns(src, core)], halves[n], own_sem.at[n])
+        copy.start()
+        local.append(copy)
+        begin(far(src.at[:, :, columns(src, 1 - core)], mates[n], send_m.at[n], recv_m.at[n], sibling, ka))
+    for m, p in enumerate(plane):
+        begin(far(gq.at[:, quarter(gq, (p // 2) % 4), :], fours_q.at[m], send_p.at[count, m], recv_p.at[count, m], p, ka))
+
+    for n in range(count):
+        local[n].wait()
+        far(mates[n], mates[n], send_m.at[n], recv_m.at[n], sibling, ka).wait_recv()
+
+        def add(z, carry, n=n):
+            halves[n][z] = (halves[n][z].astype(F32) + mates[n][z].astype(F32)).astype(BF)
+            return carry
+
+        lax.fori_loop(0, SPAN, add, 0)
+        for m, p in enumerate(plane):
+            begin(
+                far(
+                    halves[n].at[:, quarter(halves[n], (p // 2) % 4), :], fours[n].at[m],
+                    send_p.at[n, m], recv_p.at[n, m], p, ka,
+                )
+            )
+
+    for m, p in enumerate(plane):
+        far(fours_q.at[m], fours_q.at[m], send_p.at[count, m], recv_p.at[count, m], p, ka).wait_recv()
+    mine = quarter(gq, rank)
+    sum_q[...] = (
+        gq[:, mine, :].astype(F32) + fours_q[0].astype(F32) + fours_q[1].astype(F32) + fours_q[2].astype(F32)
+    ).astype(BF)
+    for i in range(1, SPAN):
+        z = (ka + i) % SPAN
+        begin(far(sum_q.at[z], zq.at[ka], send_z.at[count, i - 1], recv_z.at[count, i - 1], pb, z))
+    zq[ka] = sum_q[ka]
+
+    for n in range(count):
+        for m, p in enumerate(plane):
+            far(fours[n].at[m], fours[n].at[m], send_p.at[n, m], recv_p.at[n, m], p, ka).wait_recv()
+        held = quarter(halves[n], rank)
+
+        def add(z, carry, n=n, held=held):
+            total = halves[n][z, held, :].astype(F32)
+            for m in range(3):
+                total = total + fours[n][m, z].astype(F32)
+            sums[n][z] = total.astype(BF)
+            return carry
+
+        lax.fori_loop(0, SPAN, add, 0)
+        for i in range(1, SPAN):
+            z = (ka + i) % SPAN
+            begin(far(sums[n].at[z], zs[n].at[i - 1], send_z.at[n, i - 1], recv_z.at[n, i - 1], pb, z))
+
+    for i in range(1, SPAN):
+        z = (ka - i) % SPAN
+        far(zq.at[z], zq.at[z], send_z.at[count, i - 1], recv_z.at[count, i - 1], pb, z).wait_recv()
+    for d in range(2):
+        fin_q[d] = (zq[d].astype(F32) + zq[SPAN - 1 - d].astype(F32)).astype(BF)
+
+    for n in range(count):
+        for i in range(1, SPAN):
+            far(zs[n].at[i - 1], zs[n].at[i - 1], send_z.at[n, i - 1], recv_z.at[n, i - 1], pb, ka).wait_recv()
+        total = sums[n][ka].astype(F32)
+        for i in range(3):
+            total = total + zs[n][i].astype(F32)
+        fins[n][...] = total.astype(BF)
+
+    if outer > 1:
+        for n in range(count + 1):
+            fin = fin_q if n == count else fins[n]
+            slot = slots_q if n == count else slots[n]
+            for o, p in enumerate(beyond):
+                far(fin, slot.at[where], send_o.at[n, o], recv_o.at[n, o], p, ka).start()
+            slot[where] = fin[...]
+        for n in range(count + 1):
+            slot = slots_q if n == count else slots[n]
+            for o in range(outer - 1):
+                far(slot.at[0], slot.at[0], send_o.at[n, o], recv_o.at[n, o], pb, ka).wait_recv()
+            total = slot[0].astype(F32)
+            for o in range(1, outer):
+                total = total + slot[o].astype(F32)
+            for o in range(outer - 1):
+                far(slot.at[0], slot.at[0], send_o.at[n, o], recv_o.at[n, o], pb, ka).wait_send()
+            (fin_q if n == count else fins[n])[...] = total.astype(BF)
+
+    def piece(n, r):
+        out = outs[n]
+        return out.at[quarter(out, r), columns(out, core)]
+
+    keeps = []
+    for n in range(count):
+        copy = pltpu.make_async_copy(fins[n], piece(n, rank), keep_sem.at[n])
+        copy.start()
+        keeps.append(copy)
+        for m, p in enumerate(plane):
+            begin(far(fins[n], piece(n, rank), send_g.at[n, m], recv_g.at[n, m], p, ka))
+    rows_q = quarter(out_q, rank)
+    for d in range(2):
+        copy = pltpu.make_async_copy(fin_q.at[d], out_q.at[2 * d + core, rows_q], keep_sem.at[count + d])
+        copy.start()
+        keeps.append(copy)
+        for m, p in enumerate(plane):
+            begin(far(fin_q.at[d], out_q.at[2 * d + core, rows_q], send_g.at[count + d, m], recv_g.at[count + d, m], p, ka))
+    for copy in keeps:
+        copy.wait()
+    for n in range(count):
+        for m, p in enumerate(plane):
+            got = piece(n, (p // 2) % 4)
+            far(got, got, send_g.at[n, m], recv_g.at[n, m], p, ka).wait_recv()
+        strip = outs[n].at[:, columns(outs[n], core)]
+        begin(far(strip, strip, send_c.at[n], recv_c.at[n], sibling, ka))
+    for d in range(2):
+        for m, p in enumerate(plane):
+            got = out_q.at[2 * d + core, quarter(out_q, (p // 2) % 4)]
+            far(got, got, send_g.at[count + d, m], recv_g.at[count + d, m], p, ka).wait_recv()
+        strip = out_q.at[2 * d + core]
+        begin(far(strip, strip, send_c.at[count + d], recv_c.at[count + d], sibling, ka))
+    for n in range(count):
+        strip = outs[n].at[:, columns(outs[n], 1 - core)]
+        far(strip, strip, send_c.at[n], recv_c.at[n], sibling, ka).wait_recv()
+    for d in range(2):
+        strip = out_q.at[2 * d + 1 - core]
+        far(strip, strip, send_c.at[count + d], recv_c.at[count + d], sibling, ka).wait_recv()
+    for copy in started:
+        copy.wait_send()
+
+
+def reduce_call(parts, gq):
+    outer = lax.axis_size("pb") // 8
+    count = len(parts)
+    anyspace = pl.BlockSpec(memory_space=pl.ANY)
+    vmem = pl.BlockSpec(memory_space=pltpu.VMEM)
+    shape = jax.ShapeDtypeStruct
+    dma = pltpu.SemaphoreType.DMA
+    vm = pltpu.VMEM
+    small = [(p.shape[1] // 4, p.shape[2] // 2) for p in parts]
+    sq = (gq.shape[1] // 4, gq.shape[2])
+    beyond = max(outer - 1, 1)
+    held = outer if outer > 1 else 1
+    scratch = (
+        [vm((SPAN, p.shape[1], p.shape[2] // 2), BF) for p in parts]
+        + [vm((SPAN, p.shape[1], p.shape[2] // 2), BF) for p in parts]
+        + [vm((3, SPAN) + s, BF) for s in small]
+        + [vm((SPAN,) + s, BF) for s in small]
+        + [vm((3,) + s, BF) for s in small]
+        + [vm(s, BF) for s in small]
+        + [vm((held,) + (s if outer > 1 else (16, 128)), BF) for s in small]
+        + [
+            vm((3, SPAN) + sq, BF),
+            vm((SPAN,) + sq, BF),
+            vm((SPAN,) + sq, BF),
+            vm((2,) + sq, BF),
+            vm((held, 2) + (sq if outer > 1 else (16, 128)), BF),
+        ]
+        + [
+            dma((count,)), dma((count,)), dma((count,)), dma((count + 1, 3)), dma((count + 1, 3)),
+            dma((count + 1, 3)), dma((count + 1, 3)), dma((count + 1, beyond)), dma((count + 1, beyond)),
+            dma((count + 2, 3)), dma((count + 2, 3)), dma((count + 2,)), dma((count + 2,)), dma((count + 2,)),
+        ]
+    )
+    return pl.pallas_call(
+        functools.partial(reduce_kernel, outer, count),
+        out_shape=tuple(shape(p.shape[1:], BF) for p in parts) + (shape((SPAN,) + gq.shape[1:], BF),),
+        in_specs=[anyspace] * count + [vmem],
+        out_specs=(anyspace,) * (count + 1),
+        scratch_shapes=scratch,
+        compiler_params=pltpu.CompilerParams(
+            collective_id=2, has_side_effects=True, vmem_limit_bytes=56 << 20
+        ),
+        name="reduce_gradients",
+    )(*parts, gq)
+
+
 def normalize(values):
     center = values - jnp.mean(values, axis=1, keepdims=True)
-    spread = jnp.mean(center * center, axis=1, keepdims=True)
-    return center * lax.rsqrt(spread + 1e-05)
-
-
-def norm_gain(values, gain_vec):
-    return normalize(values) * gain_vec
+    inverse = lax.rsqrt(jnp.mean(center * center, axis=1, keepdims=True) + 1e-05)
+    return center * inverse, inverse
+
+
+def norm_back(cot, norm, inverse):
+    return inverse * (
+        cot - jnp.mean(cot, axis=1, keepdims=True) - norm * jnp.mean(cot * norm, axis=1, keepdims=True)
+    )
 
 
 def gelu_tanh(values):
     return jax.nn.gelu(values, approximate=True)
 
 
-def contract_rows(left, right):
-    return lax.dot_general(
-        left, right, (((0,), (0,)), ((), ())), preferred_element_type=jnp.float32
-    )
-
-
-def contract_cols(left, right):
-    return lax.dot_general(
-        left, right, (((1,), (1,)), ((), ())), preferred_element_type=jnp.float32
-    )
-
-
 def body(layer_input, second_start, gain_attn, w_qkv, w_out, gain_mlp, w_up, w_down, d_output):
-    row_count = layer_input.shape[0]
+    rows = layer_input.shape[0]
     kv_index = lax.axis_index("ka")
-    kv_count = lax.axis_size("ka")
-    group_rows = row_count * kv_count
-    block_rows = min(512, group_rows)
-    block_count = group_rows // block_rows
-    score_scale = 1.0 / math.sqrt(HEAD)
-    split_at = second_start[0]
-    full_qkv = lax.all_gather(w_qkv, "ka", axis=0, tiled=True)
-    inputs32 = layer_input.astype(jnp.float32)
-    attn_in = (normalize(inputs32) * gain_attn).astype(jnp.bfloat16)
+    inputs32 = layer_input.astype(F32)
+    norm_one, inverse_one = normalize(inputs32)
+    attn_in = (norm_one * gain_attn).astype(BF)
     wq4 = w_qkv.reshape(D // SPAN, 3, SPAN, WIDE).transpose(2, 0, 1, 3).reshape(SPAN, D // SPAN, 3 * WIDE)
-    start = jnp.full((8, 128), split_at, F32)
-    got = forward_call(attn_in, wq4, start, w_out, w_up, w_down)
-    full_out = got[9].reshape(D, D)
-    full_up = got[10].reshape(D, -1)
-    full_down = got[11].reshape(-1, D)
-    projected = jnp.dot(attn_in, full_qkv, preferred_element_type=jnp.float32).astype(jnp.bfloat16)
-    keys_own = projected[:, D : 2 * D].reshape(row_count, HEADS, HEAD)
-    values_own = projected[:, 2 * D :].reshape(row_count, HEADS, HEAD)
-    block_ids = jnp.arange(block_count)
-    own_pos = kv_index * row_count + jnp.arange(row_count)
-
-    def pair_scores(query_blk, query_pos, key_blk, key_pos):
-        query_side = query_pos >= split_at
-        key_side = key_pos >= split_at
-        allowed = (key_pos[None, :] <= query_pos[:, None]) & (
-            key_side[None, :] == query_side[:, None]
-        )
-        scores = (
-            jnp.einsum("qhd,khd->hqk", query_blk, key_blk, preferred_element_type=jnp.float32)
-            * score_scale
-        )
-        expo = jnp.where(allowed[None], jnp.cosh(scores), 0.0)
-        sine = jnp.where(allowed[None], jnp.sinh(scores), 0.0)
-        signed = sine.astype(jnp.bfloat16)
-        return (sine, expo, signed)
-
-    def block_scores(query_blk, block_idx):
-        query_pos = block_idx * block_rows + jnp.arange(block_rows)
-        return pair_scores(query_blk, query_pos, keys_own, own_pos)
-
-    queries_all = lax.all_gather(projected[:, :D], "ka", axis=0, tiled=True)
-    query_blocks = queries_all.reshape(block_count, block_rows, HEADS, HEAD)
-
-    def forward_block(pieces):
-        query_blk, block_idx = pieces
-        sine, expo, signed = block_scores(query_blk, block_idx)
-        partial_blk = jnp.einsum(
-            "hqk,khd->qhd", signed, values_own, preferred_element_type=jnp.float32
-        )
-        return (partial_blk.reshape(block_rows, D), jnp.sum(expo, axis=2))
-
-    partial_out, partial_sums = lax.map(forward_block, (query_blocks, block_ids))
-    partial_out = partial_out.reshape(group_rows, D)
-    partial_sums = jnp.transpose(partial_sums, (1, 0, 2)).reshape(HEADS, group_rows)
-    sums_all = lax.psum(partial_sums.astype(jnp.bfloat16), "ka").astype(jnp.float32)
-    own_out = lax.psum_scatter(
-        partial_out.astype(jnp.bfloat16), "ka", scatter_dimension=0, tiled=True
-    ).astype(jnp.float32)
-    own_sums = lax.dynamic_slice_in_dim(sums_all, kv_index * row_count, row_count, 1)
-    row_totals = own_sums.T[:, :, None]
-    attn_heads = own_out.reshape(row_count, HEADS, HEAD) / row_totals
-    attn_low = got[0].transpose(1, 0, 2).reshape(row_count, D)
-    attn_branch = jnp.dot(attn_low, full_out, preferred_element_type=jnp.float32)
+    start = jnp.full((8, 128), second_start[0].astype(F32), F32)
+    (o_home, xg, wq, q, k, v, ah, tot, starts, wo_g, wu_g, wd_g) = forward_call(
+        attn_in, wq4, start, w_out, w_up, w_down
+    )
+    full_out = wo_g.reshape(D, D)
+    full_up = wu_g.reshape(D, -1)
+    full_down = wd_g.reshape(-1, D)
+    attn_low = o_home.transpose(1, 0, 2).reshape(rows, D)
+    attn_branch = dot_nn(attn_low, full_out)
     middle = inputs32 + attn_branch
-    mlp_in = (normalize(middle) * gain_mlp).astype(jnp.bfloat16)
-    up_proj = jnp.dot(mlp_in, full_up, preferred_element_type=jnp.float32)
-    activated = gelu_tanh(up_proj).astype(jnp.bfloat16)
-    mlp_branch = jnp.dot(activated, full_down, preferred_element_type=jnp.float32)
-    output = (middle + mlp_branch).astype(jnp.bfloat16)
+    norm_two, inverse_two = normalize(middle)
+    mlp_in = (norm_two * gain_mlp).astype(BF)
+    up_proj = dot_nn(mlp_in, full_up)
+    activated = gelu_tanh(up_proj).astype(BF)
+    mlp_branch = dot_nn(activated, full_down)
+    output = (middle + mlp_branch).astype(BF)
     squares = jnp.stack(
-        [
-            jnp.sum(inputs32 * inputs32),
-            jnp.sum(attn_branch * attn_branch),
-            jnp.sum(middle * middle),
-            jnp.sum(mlp_branch * mlp_branch),
-        ]
-    )
-    d_act = contract_cols(d_output, full_down)
-    d_w_down = contract_rows(activated, d_output)
-    gelu_back = jax.vjp(gelu_tanh, up_proj)[1]
-    d_up = gelu_back(d_act)[0].astype(jnp.bfloat16)
-    d_w_up = contract_rows(mlp_in, d_up)
-    d_mlp_in = contract_cols(d_up, full_up)
-    norm_back_two = jax.vjp(norm_gain, middle, gain_mlp)[1]
-    d_middle_norm, d_gain_mlp = norm_back_two(d_mlp_in)
-    d_middle = d_output.astype(jnp.float32) + d_middle_norm
-    g_middle = d_middle.astype(jnp.bfloat16)
-    d_w_out = contract_rows(attn_low, g_middle)
-    d_attn = contract_cols(g_middle, full_out).astype(jnp.bfloat16)
-    d_attn_heads = d_attn.astype(jnp.float32).reshape(row_count, HEADS, HEAD)
-    d_mixed = (d_attn_heads / row_totals).reshape(row_count, D).astype(jnp.bfloat16)
-    row_terms = (jnp.sum(d_attn_heads * attn_heads, axis=2) / own_sums.T).T
-    mixed_all, terms_all = (
-        lax.all_gather(d_mixed, "ka", axis=0, tiled=True),
-        lax.all_gather(row_terms.astype(jnp.bfloat16), "ka", axis=1, tiled=True).astype(
-            row_terms.dtype
-        ),
-    )
-    grad_blocks = mixed_all.reshape(block_count, block_rows, HEADS, HEAD)
-    term_blocks = jnp.transpose(terms_all.reshape(HEADS, block_count, block_rows), (1, 0, 2))
-
-    def backward_block(carry, pieces):
-        key_acc, value_acc = carry
-        query_blk, grad_blk, term_blk, block_idx = pieces
-        sine, expo, signed = block_scores(query_blk, block_idx)
-        d_signed = jnp.einsum(
-            "qhd,khd->hqk", grad_blk, values_own, preferred_element_type=jnp.float32
-        )
-        d_scores = (expo * d_signed - sine * term_blk[:, :, None]).astype(jnp.bfloat16)
-        d_query = (
-            jnp.einsum("hqk,khd->qhd", d_scores, keys_own, preferred_element_type=jnp.float32)
-            * score_scale
-        )
-        key_acc = (
-            key_acc
-            + jnp.einsum("hqk,qhd->khd", d_scores, query_blk, preferred_element_type=jnp.float32)
-            * score_scale
-        )
-        value_acc = value_acc + jnp.einsum(
-            "hqk,qhd->khd", signed, grad_blk, preferred_element_type=jnp.float32
-        )
-        return ((key_acc, value_acc), d_query.reshape(block_rows, D))
-
-    zero_acc = jnp.zeros((row_count, HEADS, HEAD), jnp.float32)
-    (d_keys, d_values), query_parts = lax.scan(
-        backward_block, (zero_acc, zero_acc), (query_blocks, grad_blocks, term_blocks, block_ids)
-    )
-    d_queries = lax.psum_scatter(
-        query_parts.reshape(group_rows, D).astype(jnp.bfloat16),
-        "ka",
-        scatter_dimension=0,
-        tiled=True,
-    ).astype(jnp.float32)
-    d_projected = jnp.concatenate(
-        [d_queries, d_keys.reshape(row_count, D), d_values.reshape(row_count, D)], axis=1
-    ).astype(jnp.bfloat16)
-    d_w_qkv = contract_rows(attn_in, d_projected)
-    d_attn_in = contract_cols(d_projected, full_qkv)
-    norm_back_one = jax.vjp(norm_gain, inputs32, gain_attn)[1]
-    d_input_norm, d_gain_attn = norm_back_one(d_attn_in)
-    d_input = d_middle + d_input_norm
-    all_totals = lax.psum(
-        (
-            lax.psum_scatter(
-                d_gain_attn.astype(jnp.bfloat16), "ka", scatter_dimension=0, tiled=True
-            ).astype(jnp.float32),
-            lax.psum_scatter(
-                d_w_qkv.astype(jnp.bfloat16), "ka", scatter_dimension=0, tiled=True
-            ).astype(jnp.float32),
-            lax.psum_scatter(
-                d_w_out.astype(jnp.bfloat16), "ka", scatter_dimension=0, tiled=True
-            ).astype(jnp.float32),
-            lax.psum_scatter(
-                d_gain_mlp.astype(jnp.bfloat16), "ka", scatter_dimension=0, tiled=True
-            ).astype(jnp.float32),
-            lax.psum_scatter(
-                d_w_up.astype(jnp.bfloat16), "ka", scatter_dimension=0, tiled=True
-            ).astype(jnp.float32),
-            lax.psum_scatter(
-                d_w_down.astype(jnp.bfloat16), "ka", scatter_dimension=0, tiled=True
-            ).astype(jnp.float32),
-            lax.psum_scatter(
-                squares.astype(jnp.bfloat16), "ka", scatter_dimension=0, tiled=True
-            ).astype(jnp.float32),
-        ),
-        "pb",
-    )
-    total_gain_attn, total_qkv, total_out, total_gain_mlp, total_up, total_down, total_squares = (
-        all_totals
-    )
-    entry_count = row_count * kv_count * lax.axis_size("pb") * D
-    rms = jnp.sqrt(total_squares / entry_count)
+        [jnp.sum(t * t) for t in (inputs32, attn_branch, middle, mlp_branch)]
+    )
+    d_act = dot_nt(d_output, full_down)
+    d_w_down = dot_tn(activated, d_output).astype(BF)
+    d_up = jax.vjp(gelu_tanh, up_proj)[1](d_act)[0].astype(BF)
+    d_w_up = dot_tn(mlp_in, d_up).astype(BF)
+    d_mlp_in = dot_nt(d_up, full_up)
+    d_middle = d_output.astype(F32) + norm_back(d_mlp_in * gain_mlp, norm_two, inverse_two)
+    g_middle = d_middle.astype(BF)
+    d_w_out = dot_tn(attn_low, g_middle).astype(BF)
+    d_attn = dot_nt(g_middle, full_out).astype(BF)
+    dah = d_attn.reshape(rows, SPAN, WIDE).transpose(1, 0, 2)
+    dxh, gq = backward_call(dah, xg, wq, q, k, v, ah, tot, starts)
+    d_attn_in = (dxh[0].astype(F32) + dxh[1].astype(F32)).reshape(rows, D)
+    d_input = d_middle + norm_back(d_attn_in * gain_attn, norm_one, inverse_one)
+    extra = jnp.zeros((SPAN, D // 12, D), BF)
+    extra = extra.at[:, 0, 0].set(squares.astype(BF))
+    go = jnp.concatenate([d_w_out.reshape(SPAN, D // SPAN, D), extra], axis=1)
+    fd, fu, fo, fq = reduce_call(
+        (d_w_down.reshape(SPAN, -1, D), d_w_up.reshape(SPAN, D // SPAN, -1), go), gq
+    )
+    total_down = fd.astype(F32)
+    total_up = fu.astype(F32)
+    total_out = fo[: D // SPAN].astype(F32)
+    total_qkv = (
+        fq.reshape(SPAN, D // SPAN, 3, WIDE).transpose(1, 2, 0, 3).reshape(D // SPAN, 3 * D).astype(F32)
+    )
+
+    def gain_grad(weight, grad, gain):
+        own = lax.dynamic_slice_in_dim(gain, kv_index * (D // SPAN), D // SPAN)
+        return jnp.sum(weight.astype(F32) * grad, axis=1) / own
+
+    total_gain_attn = gain_grad(w_qkv, total_qkv, gain_attn)
+    total_gain_mlp = gain_grad(w_up, total_up, gain_mlp)
+    entry_count = rows * SPAN * lax.axis_size("pb") * D
+    rms = jnp.sqrt(fo[D // SPAN, 0:1].astype(F32) / entry_count)
     return (
-        output,
-        d_input,
-        total_gain_attn,
-        total_qkv,
-        total_out,
-        total_gain_mlp,
-        total_up,
-        total_down,
-        rms,
+        output, d_input, total_gain_attn, total_qkv, total_out, total_gain_mlp, total_up, total_down, rms,
     )
 
 
 def solution(mesh):
+    if mesh.shape["ka"] != SPAN or mesh.shape["pb"] % 8:
+        raise ValueError("unsupported mesh")
     placed = (
-        P(("pb", "ka"), None),
-        P("pb"),
-        P(),
-        P("ka", None),
-        P("ka", None),
-        P(),
-        P("ka", None),
-        P("ka", None),
+        P(("pb", "ka"), None), P("pb"), P(), P("ka", None), P("ka", None), P(), P("ka", None), P("ka", None),
         P(("pb", "ka"), None),
     )
     return jax.shard_map(
@@ -670,15 +956,8 @@
         mesh=mesh,
         in_specs=placed,
         out_specs=(
-            P(("pb", "ka"), None),
-            P(("pb", "ka"), None),
-            P("ka"),
-            P("ka", None),
-            P("ka", None),
-            P("ka"),
-            P("ka", None),
-            P("ka", None),
-            P("ka"),
+            P(("pb", "ka"), None), P(("pb", "ka"), None), P("ka"), P("ka", None), P("ka", None), P("ka"),
+            P("ka", None), P("ka", None), P("ka"),
         ),
         check_vma=False,
     )

time: 1250 us -> 443 us (0.35)
  waiting for transfers between devices: 428 us -> 0 us
  matrix products: 296 us -> 33.6 us
  blocking collectives: 187 us -> 0 us
  Pallas kernels: 184 us -> 361 us
  local copies, waits for them, and re-layouts: 87.9 us -> 19.5 us
  other arithmetic: 39.2 us -> 19.6 us
  between operations: 17.8 us -> 3.59 us
    reduce_scatter x6 -> x0, waiting for transfers between devices: 323 us -> none  [the longest x1 88.1 us: body(): lax.psum_scatter(d_w_down.astype(jnp.bfloat16), 'ka', scatter_dimension=0...]
    dot_general x40 -> x9, matrix products: 296 us -> 33.6 us  [the longest x3 11.4 us: dot_nt(): lax.dot_general(left, right, (((1,), (1,)), ((), ())), preferred_element_...]
    pallas_call x0 -> x2, Pallas kernels: none -> 218 us  [the longest x1 122 us: reduce_call(): pl.pallas_call(functools.partial(reduce_kernel, outer, count), out_shape=...]
    psum x2 -> x0, blocking collectives: 162 us -> none  [the longest x1 145 us: body(): lax.psum((lax.psum_scatter(d_gain_attn.astype(jnp.bfloat16), 'ka', scatte...]
    all_gather x3 -> x0, waiting for transfers between devices: 103 us -> none  [the longest x1 59.8 us: body(): lax.all_gather(d_mixed, 'ka', axis=0, tiled=True)]
    pallas_call x1, Pallas kernels: 184 us -> 143 us  [forward_call(): pl.pallas_call(forward_kernel, out_shape=outs, in_specs=[vmem, anyspace,...]
    while x16 -> x0, local copies, waits for them, and re-layouts: 18.1 us -> none
    reduce_sum x8 -> x6, other arithmetic: 21.3 us -> 6.74 us  [the longest x2 1.97 us: gain_grad(): return jnp.sum(weight.astype(F32) * grad, axis=1) / own]
  transfers between devices with their start and end apart: 9 -> 0, of which waited for: 8 -> 0; matrix products, arithmetic and copies ran while one was open for 8% -> 0% of each run, Pallas kernels for 15% -> 0%
where the time goes in v2:
time: 443 us; the launch traced here: 438 us
  Pallas kernels  361 us (81%)
  matrix products  33.6 us (8%)
  other arithmetic  19.6 us (4%)
  local copies, waits for them, and re-layouts  19.5 us (4%)
    pallas_call x1, Pallas kernels, forward_call(): pl.pallas_call(forward_kernel, out_shape=outs, in_specs=[vmem, anyspace,...  143 us
    pallas_call x1, Pallas kernels, reduce_call(): pl.pallas_call(functools.partial(reduce_kernel, outer, count), out_shape=...  122 us
    pallas_call x1, Pallas kernels, backward_call(): pl.pallas_call(backward_kernel, out_shape=(shape((2, 2, rows // 2, D), BF...  96.3 us
    dot_general x3, matrix products, dot_nt(): lax.dot_general(left, right, (((1,), (1,)), ((), ())), preferred_element_...  11.4 us
    dot_general x3, matrix products, dot_nn(): return jnp.dot(left, right, preferred_element_type=F32)  11.3 us
    dot_general x3, matrix products, dot_tn(): lax.dot_general(left, right, (((0,), (0,)), ((), ())), preferred_element_...  10.9 us

profile of v2, /device:TPU:0, one launch (start us, length us, event | category | flops | bytes accessed | tf_op | source)
XLA Modules:
  0.0 437.5 jit_solution(9407619896870848252)
XLA Ops:
  1.4 1.4 convert_reduce_fusion
  2.8 1.5 fusion.21
  4.9 1.2 fusion.16.xa
  6.1 1.1 reshape.194
  7.2 1.0 copy.39
  8.2 1.3 copy.40.wq4
  9.6 143.3 %forward_attention.1 = (bf16[4,512,192]{2,1,0:T(8,128)(2,1)}, bf16[4,2,256,768]{3,2,1,0:T(8,128)(2,1)}, bf16[4,192,576]{2,1,0:T(8,128)(2,1)}, bf16[3,2048,64]{2,...) custom-call(bf16[512,768]{1,0:T(8,128)(2,1)} %fusion.16.xa, ...), custom_call_target="tpu_custom_call" | custom-call | tf_op jit(solution)/shard_map/forward_attention/pallas_call | solution.py:411
  152.8 2.3 copy.45
  155.1 3.0 fusion.31
  158.8 2.7 fusion.29
  161.6 6.2 %fusion.6 = bf16[512,3072]{1,0:T(8,128)(2,1)S(1)} fusion(f32[512,3072]{1,0:T(8,128)S(1)} %fusion.29, bf16[3072,768]{1,0:T(8,128)(2,1)S(1)} %bitcast.77, bf16[512,768]{1,0:T(8,128)(2,1)S(1)} %copy-done.13), kind=kOutput, calls=%fused_computation.8 | convolution fusion | flops 2447376384 | bytes 14942208 | tf_op jit(solution)/shard_map/dot_general | solution.py:52
  167.7 3.5 multiply_reduce_fusion.3
  171.3 5.6 %multiply_reduce_fusion.2 = (bf16[]{:T(256)}, bf16[512,768]{1,0:T(8,128)(2,1)}, f32[512,768]{1,0:T(8,128)S(1)}) fusion(f32[512,768]{1,0:T(8,128)S(1)} %get-tuple-element.65, f32[512]{0:T(512)S(1)} %get-tuple-element.73, f32[512]{0:T(512)S(1)} %broadcast_multiply_fusion.3, f32[512,768]{1,0:T(8,128)S(1)} %get-tuple-element.72, f32[512]{0:T(512)S(1)} %get-tuple-element.74, ...), kind=kOutput, calls=%fused_computation.41 | convolution fusion | flops 2434793472 | bytes 17309698 | tf_op jit(solution)/shard_map/dot_general | solution.py:60
  176.8 5.4 %convolution_convert_fusion.1 = bf16[3072,768]{1,0:T(8,128)(2,1)} fusion(bf16[512,768]{1,0:T(8,128)(2,1)S(1)} %copy-done.13, f32[512,3072]{1,0:T(8,128)S(1)} %fusion.29), kind=kOutput, calls=%fused_computation.16 | convolution fusion | flops 2432434176 | bytes 11796480 | tf_op jit(solution)/shard_map/dot_general | solution.py:56
  182.2 4.8 %convolution_convert_fusion = bf16[768,3072]{1,0:T(8,128)(2,1)} fusion(bf16[512,3072]{1,0:T(8,128)(2,1)S(1)} %fusion.6, f32[512,768]{1,0:T(8,128)S(1)} %get-tuple-element.65, f32[768]{0:T(1024)S(1)} %copy-done.10, f32[512]{0:T(512)S(1)} %add_rsqrt_fusion, f32[512]{0:T(512)S(1)} %broadcast_multiply_fusion.3), kind=kOutput, calls=%fused_computation.15 | convolution fusion | flops 2419851264 | bytes 9444352 | tf_op jit(solution)/shard_map/dot_general | solution.py:56
  187.0 1.7 convolution_convert_fusion.3
  188.7 1.4 copy.43
  190.1 1.3 copy.44
  191.4 96.3 %backward_attention.1 = (bf16[2,2,256,768]{3,2,1,0:T(8,128)(2,1)}, bf16[4,192,576]{2,1,0:T(8,128)(2,1)}) custom-call(bf16[4,512,192]{2,1,0:T(8,128)(2,1)} %bitcast.70, bf16[4,2,256,768]{3,2,1,0:T(8,128)(2,1)} %get-tuple-element.43.xg_in, bf16[4,192,576]{2,1,0:T(8,128)(2,1)} %get-tuple-element.44.wq_in, bf16[3,2048,64]{2,1,0:T(8,128)(2,1)} %get-tuple-element.45.q_in, ...), custom_call_target="tpu_custom_call" | custom-call | tf_op jit(solution)/shard_map/backward_attention/pallas_call | solution.py:633
  287.8 1.7 multiply_reduce_fusion.4
  289.5 1.3 fusion.22
  290.8 2.7 pad_maximum_fusion
  293.4 1.7 fusion.20
  296.1 1.3 fusion.23.refs_2_
  297.3 121.5 %reduce_gradients.1 = (bf16[768,768]{1,0:T(8,128)(2,1)}, bf16[192,3072]{1,0:T(8,128)(2,1)}, bf16[256,768]{1,0:T(8,128)(2,1)}, bf16[4,192,576]{2,1,0:T(8,128)(2,1)}) custom-call(bf16[4,768,768]{2,1,0:T(8,128)(2,1)} %bitcast.68, bf16[4,192,3072]{2,1,0:T(8,128)(2,1)} %bitcast.69, bf16[4,256,768]{2,1,0:T(8,128)(2,1)} %fusion.23.refs_2_, ...), custom_call_target="tpu_custom_call" | custom-call | tf_op jit(solution)/shard_map/reduce_gradients/pallas_call | solution.py:853
  418.8 1.1 slice.34
  420.7 1.8 slice_convert_fusion
  422.5 1.5 copy.47
  424.0 2.5 copy.48
  426.6 2.9 reshape.204
  431.4 1.6 convert_element_type.115
  433.9 1.7 multiply_reduce_fusion
  (48 shorter events, 5.7 us)
Async XLA Ops:
  0.6 4.3 copy-start
  0.7 4.3 copy-start.9
  1.4 4.7 %copy-start.3 = (bf16[192,2304]{1,0:T(8,128)(2,1)S(1)}, bf16[192,2304]{1,0:T(8,128)(2,1)}, u32[]{:S(2)}) copy-start(bf16[192,2304]{1,0:T(8,128)(2,1)} %param.14) | copy-start | bytes 2654212
  152.8 2.3 copy-start.8
  155.1 3.3 copy-start.11
  158.1 0.7 copy-start.10
  158.1 3.4 slice-start
  158.8 2.8 slice-start.1
  158.8 2.8 copy-start.13
  182.2 4.8 %copy-start.12 = (bf16[4,192,768]{2,1,0:T(8,128)(2,1)S(1)}, bf16[4,192,768]{2,1,0:T(8,128)(2,1)}, u32[]{:S(2)}) copy-start(bf16[4,192,768]{2,1,0:T(8,128)(2,1)} %get-tuple-element.40) | copy-start | bytes 3538948
  293.4 1.7 copy-start.5
  426.6 2.9 copy-start.4
  429.5 3.5 copy-start.1
  429.5 1.9 copy-start.7
  431.4 1.7 copy-start.2
  431.4 2.5 copy-start.6

commit v3 on v2

v3 whole, which is shorter than its diff:
```python
import functools
import math

import jax
import jax.numpy as jnp
from jax import lax
from jax.experimental import pallas as pl
from jax.experimental.pallas import tpu as pltpu
from jax.sharding import PartitionSpec as P

D = 768
HEADS = 12
HEAD = 64
SPAN = 4
LOCAL = HEADS // SPAN
WIDE = LOCAL * HEAD
LOG2E = 1.4426950408889634
MESH = pl.DeviceIdType.MESH
BF = jnp.bfloat16
F32 = jnp.float32


def mirror(depth, side):
    return depth + side * (SPAN - 1 - 2 * depth)


def neighbours(pb):
    across_x = pb + 2 - 4 * ((pb // 2) % 2)
    across_y = pb + 4 - 8 * ((pb // 4) % 2)
    across_both = across_x + 4 - 8 * ((across_x // 4) % 2)
    return across_x, across_y, across_both


def sibling_of(pb):
    return pb + 1 - 2 * (pb % 2)


def far(src, dst, send_sem, recv_sem, pb, ka):
    return pltpu.make_async_remote_copy(
        src, dst, send_sem, recv_sem, device_id=(pb, ka), device_id_type=MESH
    )


def greet(peers):
    barrier = pltpu.get_barrier_semaphore()
    for peer in peers:
        pl.semaphore_signal(barrier, 1, device_id=peer, device_id_type=MESH)
    pl.semaphore_wait(barrier, len(peers))


def dot_nt(left, right):
    return lax.dot_general(left, right, (((1,), (1,)), ((), ())), preferred_element_type=F32)


def dot_tn(left, right):
    return lax.dot_general(left, right, (((0,), (0,)), ((), ())), preferred_element_type=F32)


def dot_nn(left, right):
    return jnp.dot(left, right, preferred_element_type=F32)


def fold_lanes(tile):
    out = tile[:, :128]
    for at in range(128, tile.shape[1], 128):
        out = out + tile[:, at : at + 128]
    return out


def forward_kernel(
    xa, wq4, start, wo, wu, wd,
    ohome, xg_out, wq_out, q_out, k_out, v_out, ah_out, tot_out, start_out, wog, wug, wdg,
    xg, wqs, qs, ks, vs, ahs, tots, ob, starts, wo_own, wu_own, wd_own,
    send_x, recv_x, send_q, recv_q, send_w, recv_w, send_s, recv_s, send_o, recv_o,
    send_z, recv_z, send_p, recv_p, send_c, recv_c, own_sem, out_sem,
):
    pb = lax.axis_index("pb")
    ka = lax.axis_index("ka")
    core = pb % 2
    base = pb - core
    side = ka // 2
    depth = mirror(ka, side)
    home_u = mirror(ka, core)
    quarter = 2 * depth + core
    sibling = sibling_of(pb)
    plane = neighbours(pb)
    rows = xa.shape[0]
    half = rows // 2
    rank = (pb // 2) % 4

    greet(
        [(pb, (ka + i) % SPAN) for i in range(1, SPAN)]
        + [(sibling, (ka + i) % SPAN) for i in range(SPAN)]
        + [(p, ka) for p in plane]
    )

    odd = (((home_u + 1) // 2) % 2) * (1 - home_u // 2)
    goal = mirror(1 - odd, core)
    out_x = [
        far(xa.at[pl.ds(h * half, half)], xg.at[ka, h], send_x.at[h], recv_x.at[ka, h], base + h, goal)
        for h in range(2)
    ]
    for copy in out_x:
        copy.start()

    at_home = core == side

    def near_copies():
        remote = [
            far(xa.at[pl.ds(h * half, half)], xg.at[ka, h], send_x.at[2 + h], recv_x.at[ka, h], sibling, ka)
            for h in range(2)
        ]
        local = [
            pltpu.make_async_copy(xa.at[pl.ds(h * half, half)], xg.at[ka, h], recv_x.at[ka, h])
            for h in range(2)
        ]
        return remote, local

    @pl.when(at_home)
    def _():
        remote, local = near_copies()
        for copy in remote + local:
            copy.start()

    def start_copies():
        out = []
        for n, (d, k) in enumerate(((0, 1), (1, 0), (1, 1))):
            target = base + (core + k) % 2
            out.append(far(start, starts, send_s.at[n], recv_s, target, mirror(d, core)))
        return out

    @pl.when(home_u == 0)
    def _():
        for copy in start_copies():
            copy.start()
        pltpu.make_async_copy(start, starts, recv_s).start()

    height = wq4.shape[1] // 4

    def lines(ref, r):
        return ref.at[pl.ds(pl.multiple_of(r * height, 16), height)]

    out_q = []
    for i in range(1, SPAN):
        z = (ka + i) % SPAN
        zd = mirror(z, z // 2)
        out_q.append(
            far(
                lines(wq4.at[2 * zd + core], rank), lines(wqs.at[ka], rank),
                send_q.at[i - 1], recv_q.at[i - 1], pb, z,
            )
        )
    for copy in out_q:
        copy.start()
    own_q = pltpu.make_async_copy(wq4.at[quarter], wqs.at[ka], own_sem.at[0])
    own_q.start()
    own_w = [
        pltpu.make_async_copy(src, dst, own_sem.at[1 + n])
        for n, (src, dst) in enumerate(((wo, wo_own), (wu, wu_own), (wd, wd_own)))
    ]

    spread = []
    for i in range(3):
        u = (1 - depth) if i == 0 else i + 1
        b = mirror(u, side)
        far(xg.at[b, core], xg.at[b, core], send_x.at[4], recv_x.at[b, core], pb, ka).wait_recv()
        copy = far(xg.at[b, core], xg.at[b, core], send_x.at[4 + i], recv_x.at[b, core], sibling, ka)
        copy.start()
        spread.append(copy)
        if i >= 1:
            onward = far(
                xg.at[b, core], xg.at[b, core], send_x.at[6 + i], recv_x.at[b, core], pb, mirror(0, side)
            )

            @pl.when(depth == 1)
            def _():
                onward.start()

            spread.append(onward)
        if i == 0:
            for n in range(1, SPAN):
                mine_q = lines(wqs.at[(ka - n) % SPAN], rank)
                far(mine_q, mine_q, send_q.at[0], recv_q.at[n - 1], pb, ka).wait_recv()
                for m, p in enumerate(plane):
                    copy = far(mine_q, mine_q, send_w.at[n - 1, m], recv_w.at[n - 1, m], p, ka)
                    copy.start()
                    out_q.append(copy)
    b_near = ka
    for h in range(2):
        far(xg.at[b_near, h], xg.at[b_near, h], send_x.at[4], recv_x.at[b_near, h], pb, ka).wait_recv()
    for i in range(3):
        u = (1 - depth) if i == 0 else i + 1
        b = mirror(u, side)
        far(xg.at[b, 1 - core], xg.at[b, 1 - core], send_x.at[4], recv_x.at[b, 1 - core], pb, ka).wait_recv()

    parts = (
        (wd, wdg, wd.shape[0] // 4, wd.shape[1] // 2),
        (wu, wug, wu.shape[0] // 4, wu.shape[1] // 2),
        (wo, wog, wo.shape[0] // 4, wo.shape[1] // 2),
    )

    def piece(ref, n):
        _, _, r, c = parts[n]
        return ref.at[pl.ds(pl.multiple_of(rank * r, 16), r), pl.ds(pl.multiple_of(core * c, 128), c)]

    def strip(ref, n):
        _, _, _, c = parts[n]
        return ref.at[:, pl.ds(pl.multiple_of(core * c, 128), c)]

    def strip_other(ref, n):
        _, _, _, c = parts[n]
        return ref.at[:, pl.ds(pl.multiple_of((1 - core) * c, 128), c)]

    along_z = []
    for n, (src, dst, _, _) in enumerate(parts):
        for i in range(1, SPAN):
            z = (ka + i) % SPAN
            along_z.append(
                far(piece(src, n), piece(dst.at[ka], n), send_z.at[n, i - 1], recv_z.at[n, i - 1], pb, z)
            )
    for copy in along_z + own_w:
        copy.start()

    for i in range(1, SPAN):
        for m, p in enumerate(plane):
            theirs = lines(wqs.at[(ka - i) % SPAN], (p // 2) % 4)
            far(theirs, theirs, send_w.at[i - 1, m], recv_w.at[i - 1, m], p, ka).wait_recv()
    own_q.wait()
    pltpu.make_async_copy(start, starts, recv_s).wait()

    def project(b, carry):
        xb = xg[b].reshape(rows, D)
        at = pl.multiple_of(b * rows, rows)
        for dst, col in ((qs, 0), (ks, WIDE), (vs, 2 * WIDE)):
            w = wqs[:, :, col : col + WIDE].reshape(D, WIDE)
            out = dot_nn(xb, w).astype(BF)
            for h in range(LOCAL):
                dst[h, pl.ds(at, rows), :] = out[:, h * HEAD : (h + 1) * HEAD]
        return carry

    lax.fori_loop(0, SPAN, project, 0)

    in_plane = []

    def part_of(n, i, r):
        dst, height, width = parts[n][1:]
        return dst.at[
            (ka - i) % SPAN, pl.ds(pl.multiple_of(r * height, 16), height),
            pl.ds(pl.multiple_of(core * width, 128), width),
        ]

    def plane_copy(n, i, m, r, p):
        ref = part_of(n, i, r)
        return far(ref, ref, send_p.at[n, i - 1, m], recv_p.at[n, i - 1, m], p, ka)

    def begin_plane(n):
        for i in range(1, SPAN):
            ref = part_of(n, i, rank)
            far(ref, ref, send_z.at[n, 0], recv_z.at[n, i - 1], pb, ka).wait_recv()
            for m in range(2):
                copy = plane_copy(n, i, m, rank, plane[m])
                copy.start()
                in_plane.append(copy)

    def pass_on(n):
        first = n % 2
        r = (plane[first] // 2) % 4
        for i in range(1, SPAN):
            plane_copy(n, i, first, r, pb).wait_recv()
            copy = plane_copy(n, i, 2, r, plane[1 - first])
            copy.start()
            in_plane.append(copy)

    across = []

    def begin_across(n):
        other = 1 - n % 2
        dst = parts[n][1]
        for i in range(1, SPAN):
            plane_copy(n, i, other, (plane[other] // 2) % 4, pb).wait_recv()
            plane_copy(n, i, 2, (plane[2] // 2) % 4, pb).wait_recv()
            z = (ka - i) % SPAN
            copy = far(
                strip(dst.at[z], n), strip(dst.at[z], n), send_c.at[n, i - 1], recv_c.at[n, i - 1], sibling, ka
            )
            copy.start()
            across.append(copy)

    scale = LOG2E / math.sqrt(HEAD)
    one = starts[0:1, 0:1] > (SPAN // 2) * rows + 0.5
    sub = 256

    def attend_block(b, after=()):
        for h in range(LOCAL):
            for part in range(rows // sub):
                row0 = b * rows + part * sub
                q = qs[h, row0 : row0 + sub, :]

                def full(kb, state, q=q, h=h):
                    acc, tot = state
                    at = pl.multiple_of(kb * rows, rows)
                    s = dot_nt(q, ks[h, pl.ds(at, rows), :]) * scale
                    up, down = jnp.exp2(s - 1.0), jnp.exp2(-s - 1.0)
                    tot = tot + fold_lanes(up + down)
                    acc = acc + dot_nn((up - down).astype(BF), vs[h, pl.ds(at, rows), :])
                    return acc, tot

                state = (jnp.zeros((sub, HEAD), F32), jnp.zeros((sub, 128), F32))
                if b >= SPAN // 2:
                    acc, tot = lax.fori_loop(0, SPAN // 2, full, state)
                    state = (jnp.where(one, acc, 0.0), jnp.where(one, tot, 0.0))
                    state = lax.fori_loop(SPAN // 2, b, full, state)
                else:
                    state = lax.fori_loop(0, b, full, state)
                acc, tot = state
                width = (part + 1) * sub
                s = dot_nt(q, ks[h, b * rows : b * rows + width, :]) * scale
                seen = (
                    lax.broadcasted_iota(jnp.int32, (sub, width), 0) + part * sub
                    >= lax.broadcasted_iota(jnp.int32, (sub, width), 1)
                )
                up = jnp.where(seen, jnp.exp2(s - 1.0), 0.0)
                down = jnp.where(seen, jnp.exp2(-s - 1.0), 0.0)
                tot = tot + fold_lanes(up + down)
                acc = acc + dot_nn((up - down).astype(BF), vs[h, b * rows : b * rows + width, :])
                total = jnp.sum(tot, axis=1, keepdims=True)
                heads = acc / total
                ahs[h, row0 : row0 + sub, :] = heads
                tots[h, row0 : row0 + sub, :] = jnp.broadcast_to(total, (sub, HEAD))
            for step in after[h : h + 1]:
                step()

    send_back = []
    hooks = {3: (functools.partial(begin_plane, 0), functools.partial(begin_plane, 1))}
    for b in range(SPAN):
        attend_block(b, hooks.get(b, ()))
        joined = jnp.concatenate(
            [ahs[h, b * rows : (b + 1) * rows, :] for h in range(LOCAL)], axis=1
        )
        ob[b] = joined.astype(BF)
        remote = far(ob.at[b], ohome.at[quarter], send_o.at[b], recv_o.at[quarter], base + side, b)
        mine = (core == side) & (ka == b)

        @pl.when(jnp.logical_not(mine))
        def _():
            remote.start()

        @pl.when(mine)
        def _():
            pltpu.make_async_copy(ob.at[b], ohome.at[quarter], recv_o.at[quarter]).start()

        send_back.append((mine, remote))

    for copy in own_w:
        copy.wait()
    begin_plane(2)
    for n in range(3):
        pass_on(n)
    for n in range(3):
        begin_across(n)
    saves = [
        pltpu.make_async_copy(src, dst, out_sem.at[n])
        for n, (src, dst) in enumerate(
            (
                (xg, xg_out), (wqs, wq_out), (qs, q_out), (ks, k_out), (vs, v_out),
                (ahs, ah_out), (tots, tot_out), (starts, start_out),
                (wo_own, wog.at[ka]), (wu_own, wug.at[ka]), (wd_own, wdg.at[ka]),
            )
        )
    ]
    for copy in saves:
        copy.start()

    for i in range(1, SPAN):
        z = (ka - i) % SPAN
        for n, (src, dst, _, _) in enumerate(parts):
            far(
                strip_other(dst.at[z], n), strip_other(dst.at[z], n),
                send_c.at[n, 0], recv_c.at[n, i - 1], pb, ka,
            ).wait_recv()
    for n in range(SPAN):
        far(ob.at[0], ohome.at[n], send_o.at[0], recv_o.at[n], pb, ka).wait_recv()
    for copy in saves:
        copy.wait()
    for copy in out_x + out_q + along_z + in_plane + across:
        copy.wait_send()
    for n in range(3):
        spread[(0, 1, 3)[n]].wait_send()

    @pl.when(depth == 1)
    def _():
        spread[2].wait_send()
        spread[4].wait_send()

    @pl.when(at_home)
    def _():
        remote, _ = near_copies()
        for copy in remote:
            copy.wait_send()

    @pl.when(home_u == 0)
    def _():
        for copy in start_copies():
            copy.wait_send()

    for mine, remote in send_back:

        @pl.when(jnp.logical_not(mine))
        def _():
            remote.wait_send()


def forward_call(xa, wq4, start, wo, wu, wd):
    rows = xa.shape[0]
    group = rows * SPAN
    anyspace = pl.BlockSpec(memory_space=pl.ANY)
    vmem = pl.BlockSpec(memory_space=pltpu.VMEM)
    shape = jax.ShapeDtypeStruct
    dma = pltpu.SemaphoreType.DMA
    outs = (
        shape((SPAN, rows, WIDE), BF),
        shape((SPAN, 2, rows // 2, D), BF),
        shape((SPAN, D // SPAN, 3 * WIDE), BF),
        shape((LOCAL, group, HEAD), BF),
        shape((LOCAL, group, HEAD), BF),
        shape((LOCAL, group, HEAD), BF),
        shape((LOCAL, group, HEAD), F32),
        shape((LOCAL, group, HEAD), F32),
        shape((8, 128), F32),
        shape((SPAN,) + wo.shape, BF),
        shape((SPAN,) + wu.shape, BF),
        shape((SPAN,) + wd.shape, BF),
    )
    vm = pltpu.VMEM
    scratch = [
        vm((SPAN, 2, rows // 2, D), BF),
        vm((SPAN, D // SPAN, 3 * WIDE), BF),
        vm((LOCAL, group, HEAD), BF),
        vm((LOCAL, group, HEAD), BF),
        vm((LOCAL, group, HEAD), BF),
        vm((LOCAL, group, HEAD), F32),
        vm((LOCAL, group, HEAD), F32),
        vm((SPAN, rows, WIDE), BF),
        vm((8, 128), F32),
        vm(wo.shape, BF),
        vm(wu.shape, BF),
        vm(wd.shape, BF),
        dma((9,)), dma((SPAN, 2)), dma((3,)), dma((3,)), dma((3, 3)), dma((3, 3)), dma((3,)), dma,
        dma((SPAN,)), dma((SPAN,)),
        dma((3, 3)), dma((3, 3)), dma((3, 3, 3)), dma((3, 3, 3)), dma((3, 3)), dma((3, 3)), dma((4,)), dma((11,)),
    ]
    return pl.pallas_call(
        forward_kernel,
        out_shape=outs,
        in_specs=[vmem, anyspace, vmem, anyspace, anyspace, anyspace],
        out_specs=(anyspace,) * len(outs),
        scratch_shapes=scratch,
        compiler_params=pltpu.CompilerParams(
            collective_id=0, has_side_effects=True, vmem_limit_bytes=56 << 20
        ),
        name="forward_attention",
    )(xa, wq4, start, wo, wu, wd)


CHUNKS = (
    (0, 0, 384, 0, 384),
    (0, 384, 384, 0, 384),
    (1, 0, 192, 0, 768),
    (1, 0, 192, 768, 768),
    (2, 0, 256, 0, 384),
)


def backward_kernel(
    outer, dah, xg_in, wq_in, q_in, k_in, v_in, ah_in, tot_in, starts, gd, gu, go,
    dxh, fd, fu, fo, fq,
    da, xg, wqs, qs, ks, vs, ahs, tots, dms, deltas, dqs, dp, own, mate, back, gq,
    *refs,
):
    count = len(CHUNKS)
    halves, mates, fours, sums, zs, fins, slots = (refs[i * count : (i + 1) * count] for i in range(7))
    refs = refs[7 * count :]
    fours_q, sum_q, zq, fin_q, slots_q = refs[:5]
    (
        send_a, recv_a, send_m, recv_m, send_h, recv_h, in_sem,
        own_sem, send_n, recv_n, send_p, recv_p, send_z, recv_z, send_o, recv_o,
        send_g, recv_g, send_c, recv_c, keep_sem,
    ) = refs[5:]
    pb = lax.axis_index("pb")
    ka = lax.axis_index("ka")
    core = pb % 2
    base = pb - core
    side = ka // 2
    depth = mirror(ka, side)
    sibling = sibling_of(pb)
    plane = neighbours(pb)
    rank = (pb // 2) % 4
    where = pb // 8
    beyond = [(pb + 8 * o) % (8 * outer) for o in range(1, outer)]
    rows = dah.shape[1]
    half = rows // 2

    greet(
        [(pb, (ka + i) % SPAN) for i in range(1, SPAN)]
        + [(sibling, (ka + i) % SPAN) for i in range(SPAN)]
        + [(p, ka) for p in plane]
        + [(p, ka) for p in beyond]
    )

    def outgoing(n):
        worker_depth, worker_core = n // 2, n % 2
        target, spot = base + worker_core, mirror(worker_depth, core)
        mine = (target == pb) & (spot == ka)
        return mine, far(dah.at[n], da.at[ka], send_a.at[n], recv_a.at[ka], target, spot)

    for n in range(SPAN):
        mine, remote = outgoing(n)

        @pl.when(jnp.logical_not(mine))
        def _():
            remote.start()

        @pl.when(mine)
        def _():
            pltpu.make_async_copy(dah.at[n], da.at[ka], recv_a.at[ka]).start()

    sources = (gd, gu, go)
    results = (fd, fu, fo)

    def block_of(ref, n, k, row0, height):
        _, _, _, col0, width = CHUNKS[n]
        at = pl.multiple_of(k * (ref.shape[-1] // 2) + col0, 128)
        return pl.ds(row0, height), pl.ds(at, width)

    def source(n, k):
        a, row0, height, _, _ = CHUNKS[n]
        r, c = block_of(sources[a], n, k, row0, height)
        return sources[a].at[:, r, c]

    def quarter(n, r):
        height = CHUNKS[n][2] // 4
        return pl.ds(pl.multiple_of(r * height, 16), height)

    def landing(n, r):
        a, row0, height, _, _ = CHUNKS[n]
        rr, c = block_of(results[a], n, core, pl.multiple_of(row0 + r * (height // 4), 16), height // 4)
        return results[a].at[rr, c]

    def strip(n, k):
        a, row0, height, _, _ = CHUNKS[n]
        r, c = block_of(results[a], n, k, row0, height)
        return results[a].at[r, c]

    def local_half(n):
        return pltpu.make_async_copy(source(n, core), halves[n], own_sem.at[n])

    def to_sibling(n):
        return far(source(n, 1 - core), mates[n], send_n.at[n], recv_n.at[n], sibling, ka)

    def to_plane(n, m):
        p = plane[m]
        return far(
            halves[n].at[:, quarter(n, (p // 2) % 4), :], fours[n].at[m], send_p.at[n, m], recv_p.at[n, m], p, ka
        )

    def to_owner(n, i):
        z = (ka + i) % SPAN
        return far(sums[n].at[z], zs[n].at[i - 1], send_z.at[n, i - 1], recv_z.at[n, i - 1], pb, z)

    def keep(n):
        return pltpu.make_async_copy(fins[n], landing(n, rank), keep_sem.at[n])

    def to_all(n, m):
        return far(fins[n], landing(n, rank), send_g.at[n, m], recv_g.at[n, m], plane[m], ka)

    def to_twin(n):
        return far(strip(n, core), strip(n, core), send_c.at[n], recv_c.at[n], sibling, ka)

    def merge_sibling(n):
        local_half(n).wait()
        to_sibling(n).wait_recv()

        def add(z, carry):
            halves[n][z] = (halves[n][z].astype(F32) + mates[n][z].astype(F32)).astype(BF)
            return carry

        lax.fori_loop(0, SPAN, add, 0)
        for m in range(3):
            to_plane(n, m).start()

    def merge_plane(n):
        for m in range(3):
            to_plane(n, m).wait_recv()
        held = quarter(n, rank)

        def add(z, carry):
            total = halves[n][z, held, :].astype(F32)
            for m in range(3):
                total = total + fours[n][m, z].astype(F32)
            sums[n][z] = total.astype(BF)
            return carry

        lax.fori_loop(0, SPAN, add, 0)
        for i in range(1, SPAN):
            to_owner(n, i).start()

    def merge_beyond(fin, slot, n):
        for o, p in enumerate(beyond):
            far(fin, slot.at[where], send_o.at[n, o], recv_o.at[n, o], p, ka).start()
        slot[where] = fin[...]
        for o in range(outer - 1):
            far(slot.at[0], slot.at[0], send_o.at[n, o], recv_o.at[n, o], pb, ka).wait()
        total = slot[0].astype(F32)
        for o in range(1, outer):
            total = total + slot[o].astype(F32)
        fin[...] = total.astype(BF)

    def merge_z(n):
        for i in range(1, SPAN):
            to_owner(n, i).wait_recv()
        total = sums[n][ka].astype(F32)
        for i in range(3):
            total = total + zs[n][i].astype(F32)
        fins[n][...] = total.astype(BF)
        if outer > 1:
            merge_beyond(fins[n], slots[n], n)
        keep(n).start()
        for m in range(3):
            to_all(n, m).start()

    def pass_twin(n):
        keep(n).wait()
        for m in range(3):
            got = landing(n, (plane[m] // 2) % 4)
            far(got, got, send_g.at[n, m], recv_g.at[n, m], pb, ka).wait_recv()
        to_twin(n).start()

    def finish(n):
        got = strip(n, 1 - core)
        far(got, got, send_c.at[n], recv_c.at[n], sibling, ka).wait_recv()
        to_sibling(n).wait_send()
        for m in range(3):
            to_plane(n, m).wait_send()
            to_all(n, m).wait_send()
        for i in range(1, SPAN):
            to_owner(n, i).wait_send()
        to_twin(n).wait_send()

    for n in range(count):
        local_half(n).start()
        to_sibling(n).start()

    loads = [
        pltpu.make_async_copy(src, dst, in_sem.at[n])
        for n, (src, dst) in enumerate(
            (
                (q_in, qs), (k_in, ks), (v_in, vs), (ah_in, ahs), (tot_in, tots), (xg_in, xg), (wq_in, wqs),
            )
        )
    ]
    for copy in loads:
        copy.start()

    for n in range(count):
        merge_sibling(n)

    for copy in loads[:5]:
        copy.wait()
    for b in range(SPAN):
        far(dah.at[0], da.at[b], send_a.at[0], recv_a.at[b], pb, ka).wait_recv()

    scale = LOG2E / math.sqrt(HEAD)
    unit = 1.0 / math.sqrt(HEAD)
    one = jnp.where(starts[0:1, 0:1] > (SPAN // 2) * rows + 0.5, 1.0, 0.0)
    sub = 256

    for b in range(SPAN):
        block = da[b].astype(F32)
        for h in range(LOCAL):
            rows_b = slice(b * rows, (b + 1) * rows)
            scaled = block[:, h * HEAD : (h + 1) * HEAD] / tots[h, rows_b, :]
            dms[h, rows_b, :] = scaled.astype(BF)
            deltas[h, :, rows_b] = lax.dot_general(
                jnp.ones((8, HEAD), F32), scaled * ahs[h, rows_b, :],
                (((1,), (1,)), ((), ())), precision=lax.Precision.HIGHEST, preferred_element_type=F32,
            )

    def piece(i, carry):
        h = i // SPAN
        kb = i % SPAN

        @pl.when(kb == 0)
        def _():
            dqs[...] = jnp.zeros_like(dqs)

        for part in range(rows // sub):
            at = pl.multiple_of(kb * rows + part * sub, sub)
            keys = ks[h, pl.ds(at, sub), :]
            values = vs[h, pl.ds(at, sub), :]

            def terms(row0, width):
                q = qs[h, pl.ds(row0, width), :]
                dm = dms[h, pl.ds(row0, width), :]
                s = dot_nt(keys, q) * scale
                up, down = jnp.exp2(s - 1.0), jnp.exp2(-s - 1.0)
                dsig = dot_nt(values, dm)
                delta = deltas[h, 0:1, pl.ds(row0, width)]
                return q, dm, up, down, dsig, delta

            def use(q, dm, expo, sine, dsig, delta):
                ds = (expo * dsig - sine * delta).astype(BF)
                return dot_nn(ds, q), dot_nn(sine.astype(BF), dm), dot_tn(ds, keys)

            width = rows - part * sub
            q, dm, up, down, dsig, delta = terms(at, width)
            seen = lax.broadcasted_iota(jnp.int32, (sub, width), 0) <= lax.broadcasted_iota(
                jnp.int32, (sub, width), 1
            )
            up = jnp.where(seen, up, 0.0)
            down = jnp.where(seen, down, 0.0)
            dk, dv, dq = use(q, dm, up + down, up - down, dsig, delta)
            dqs[pl.ds(at, width), :] += dq

            def later(qb, state):
                dk, dv = state
                row0 = pl.multiple_of(qb * rows, rows)
                q, dm, up, down, dsig, delta = terms(row0, rows)
                dk1, dv1, dq1 = use(q, dm, up + down, up - down, dsig, delta)
                same = jnp.where(qb // 2 == kb // 2, 1.0, 0.0)
                keep_it = jnp.maximum(one, same) > 0.5
                dqs[pl.ds(row0, rows), :] += jnp.where(keep_it, dq1, 0.0)
                return dk + jnp.where(keep_it, dk1, 0.0), dv + jnp.where(keep_it, dv1, 0.0)

            dk, dv = lax.fori_loop(kb + 1, SPAN, later, (dk, dv))
            ks_out = pl.ds(at, sub)
            dp[1, h, ks_out, :] = (dk * unit).astype(BF)
            dp[2, h, ks_out, :] = dv.astype(BF)

        @pl.when(kb == SPAN - 1)
        def _():
            dp[0, h] = (dqs[...] * unit).astype(BF)

        for at_piece, step, n in HOOKS:

            @pl.when(i == at_piece)
            def _(step=step, n=n):
                steps[step](n)

        return carry

    steps = {"plane": merge_plane, "z": merge_z, "twin": pass_twin}
    lax.fori_loop(0, LOCAL * SPAN, piece, 0)

    loads[5].wait()
    loads[6].wait()
    weight = wqs[...].reshape(D, 3 * WIDE)

    def joined(b):
        rows_b = slice(b * rows, (b + 1) * rows)
        return jnp.concatenate(
            [dp[part, h, rows_b, :] for part in range(3) for h in range(LOCAL)], axis=1
        )

    def home_copy(b):
        return far(back.at[b], dxh.at[depth, core], send_h.at[b], recv_h.at[depth, core], base + side, b)

    def swap(b):
        return far(own.at[b, 1 - core], mate.at[b], send_m.at[b], recv_m.at[b], sibling, ka)

    grad = dot_tn(xg[0].reshape(rows, D), joined(0))
    for b in range(1, SPAN):
        grad = grad + dot_tn(xg[b].reshape(rows, D), joined(b))
    gq[...] = grad.astype(BF).reshape(gq.shape)
    height_q = gq.shape[1] // 4

    def lines(r):
        return pl.ds(pl.multiple_of(r * height_q, 16), height_q)

    def q_plane(m):
        p = plane[m]
        return far(
            gq.at[:, lines((p // 2) % 4), :], fours_q.at[m], send_p.at[count, m], recv_p.at[count, m], p, ka
        )

    def q_owner(i):
        z = (ka + i) % SPAN
        return far(sum_q.at[z], zq.at[ka], send_z.at[count, i - 1], recv_z.at[count, i - 1], pb, z)

    def q_landing(d, r):
        return fq.at[2 * d + core, lines(r)]

    def q_all(d, m):
        return far(fin_q.at[d], q_landing(d, rank), send_g.at[count + d, m], recv_g.at[count + d, m], plane[m], ka)

    def q_twin(d):
        ref = fq.at[2 * d + core]
        return far(ref, ref, send_c.at[count + d], recv_c.at[count + d], sibling, ka)

    for m in range(3):
        q_plane(m).start()

    for b in range(SPAN):
        own[b] = dot_nt(joined(b), weight).astype(BF).reshape(2, half, D)
        swap(b).start()

    for b in range(SPAN):
        swap(b).wait_recv()
        back[b] = (own[b, core].astype(F32) + mate[b].astype(F32)).astype(BF)
        mine = (core == side) & (ka == b)

        @pl.when(jnp.logical_not(mine))
        def _():
            home_copy(b).start()

        @pl.when(mine)
        def _():
            pltpu.make_async_copy(back.at[b], dxh.at[depth, core], recv_h.at[depth, core]).start()

    done = {(step, n) for _, step, n in HOOKS}

    def rest(step):
        for n in range(count):
            if (step, n) not in done:
                steps[step](n)

    rest("plane")
    for m in range(3):
        q_plane(m).wait_recv()
    mine_q = lines(rank)
    sum_q[...] = (
        gq[:, mine_q, :].astype(F32) + fours_q[0].astype(F32) + fours_q[1].astype(F32) + fours_q[2].astype(F32)
    ).astype(BF)
    for i in range(1, SPAN):
        q_owner(i).start()
    zq[ka] = sum_q[ka]
    rest("z")
    for i in range(1, SPAN):
        z = (ka - i) % SPAN
        far(zq.at[z], zq.at[z], send_z.at[count, i - 1], recv_z.at[count, i - 1], pb, z).wait_recv()
    for d in range(2):
        fin_q[d] = (zq[d].astype(F32) + zq[SPAN - 1 - d].astype(F32)).astype(BF)
    if outer > 1:
        merge_beyond(fin_q, slots_q, count)
    q_keep = [pltpu.make_async_copy(fin_q.at[d], q_landing(d, rank), keep_sem.at[count + d]) for d in range(2)]
    for d in range(2):
        q_keep[d].start()
        for m in range(3):
            q_all(d, m).start()
    rest("twin")
    for d in range(2):
        q_keep[d].wait()
        for m in range(3):
            got = q_landing(d, (plane[m] // 2) % 4)
            far(got, got, send_g.at[count + d, m], recv_g.at[count + d, m], pb, ka).wait_recv()
        q_twin(d).start()
    for d in range(2):
        got = fq.at[2 * d + 1 - core]
        far(got, got, send_c.at[count + d], recv_c.at[count + d], sibling, ka).wait_recv()
    for n in range(count):
        finish(n)
    for d in range(2):
        for k in range(2):
            far(back.at[0], dxh.at[d, k], send_h.at[0], recv_h.at[d, k], pb, ka).wait_recv()
    for m in range(3):
        q_plane(m).wait_send()
        for d in range(2):
            q_all(d, m).wait_send()
    for i in range(1, SPAN):
        q_owner(i).wait_send()
    for d in range(2):
        q_twin(d).wait_send()
    for n in range(SPAN):
        swap(n).wait_send()
        mine, remote = outgoing(n)

        @pl.when(jnp.logical_not(mine))
        def _():
            remote.wait_send()

        mine_b = (core == side) & (ka == n)

        @pl.when(jnp.logical_not(mine_b))
        def _():
            home_copy(n).wait_send()


HOOKS = (
    (1, "plane", 0),
    (4, "plane", 1),
    (5, "z", 0),
    (7, "plane", 2),
    (8, "z", 1),
    (8, "twin", 0),
    (10, "plane", 3),
    (11, "z", 2),
    (11, "twin", 1),
)


def backward_call(dah, xg, wq, q, k, v, ah, tot, starts, gd, gu, go):
    outer = lax.axis_size("pb") // 8
    rows = dah.shape[1]
    group = rows * SPAN
    count = len(CHUNKS)
    anyspace = pl.BlockSpec(memory_space=pl.ANY)
    vmem = pl.BlockSpec(memory_space=pltpu.VMEM)
    shape = jax.ShapeDtypeStruct
    dma = pltpu.SemaphoreType.DMA
    vm = pltpu.VMEM
    big = [(h, w) for _, _, h, _, w in CHUNKS]
    small = [(h // 4, w) for h, w in big]
    sq = (wq.shape[1] // 4, wq.shape[2])
    beyond = max(outer - 1, 1)
    held = max(outer, 1)
    spare = (16, 128)
    scratch = (
        [
            vm((SPAN, rows, WIDE), BF),
            vm(xg.shape, BF),
            vm(wq.shape, BF),
            vm(q.shape, BF),
            vm(q.shape, BF),
            vm(q.shape, BF),
            vm(q.shape, F32),
            vm(q.shape, F32),
            vm(q.shape, BF),
            vm((LOCAL, 8, group), F32),
            vm((group, HEAD), F32),
            vm((3, LOCAL, group, HEAD), BF),
            vm((SPAN, 2, rows // 2, D), BF),
            vm((SPAN, rows // 2, D), BF),
            vm((SPAN, rows // 2, D), BF),
            vm(wq.shape, BF),
        ]
        + [vm((SPAN,) + s, BF) for s in big]
        + [vm((SPAN,) + s, BF) for s in big]
        + [vm((3, SPAN) + s, BF) for s in small]
        + [vm((SPAN,) + s, BF) for s in small]
        + [vm((3,) + s, BF) for s in small]
        + [vm(s, BF) for s in small]
        + [vm((held,) + (s if outer > 1 else spare), BF) for s in small]
        + [
            vm((3, SPAN) + sq, BF),
            vm((SPAN,) + sq, BF),
            vm((SPAN,) + sq, BF),
            vm((2,) + sq, BF),
            vm((held, 2) + (sq if outer > 1 else spare), BF),
        ]
        + [
            dma((SPAN,)), dma((SPAN,)), dma((SPAN,)), dma((SPAN,)), dma((SPAN,)), dma((2, 2)), dma((7,)),
            dma((count,)), dma((count,)), dma((count,)), dma((count + 1, 3)), dma((count + 1, 3)),
            dma((count + 1, 3)), dma((count + 1, 3)), dma((count + 1, beyond)), dma((count + 1, beyond)),
            dma((count + 2, 3)), dma((count + 2, 3)), dma((count + 2,)), dma((count + 2,)), dma((count + 2,)),
        ]
    )
    return pl.pallas_call(
        functools.partial(backward_kernel, outer),
        out_shape=(
            shape((2, 2, rows // 2, D), BF),
            shape(gd.shape[1:], BF),
            shape(gu.shape[1:], BF),
            shape(go.shape[1:], BF),
            shape(wq.shape, BF),
        ),
        in_specs=[anyspace] * 8 + [vmem] + [anyspace] * 3,
        out_specs=(anyspace,) * 5,
        scratch_shapes=scratch,
        compiler_params=pltpu.CompilerParams(
            collective_id=1, has_side_effects=True, vmem_limit_bytes=60 << 20
        ),
        name="backward_attention",
    )(dah, xg, wq, q, k, v, ah, tot, starts, gd, gu, go)


def normalize(values):
    center = values - jnp.mean(values, axis=1, keepdims=True)
    inverse = lax.rsqrt(jnp.mean(center * center, axis=1, keepdims=True) + 1e-05)
    return center * inverse, inverse


def norm_back(cot, norm, inverse):
    return inverse * (
        cot - jnp.mean(cot, axis=1, keepdims=True) - norm * jnp.mean(cot * norm, axis=1, keepdims=True)
    )


def gelu_tanh(values):
    return jax.nn.gelu(values, approximate=True)


def body(layer_input, second_start, gain_attn, w_qkv, w_out, gain_mlp, w_up, w_down, d_output):
    rows = layer_input.shape[0]
    kv_index = lax.axis_index("ka")
    inputs32 = layer_input.astype(F32)
    norm_one, inverse_one = normalize(inputs32)
    attn_in = (norm_one * gain_attn).astype(BF)
    wq4 = w_qkv.reshape(D // SPAN, 3, SPAN, WIDE).transpose(2, 0, 1, 3).reshape(SPAN, D // SPAN, 3 * WIDE)
    start = jnp.full((8, 128), second_start[0].astype(F32), F32)
    (o_home, xg, wq, q, k, v, ah, tot, starts, wo_g, wu_g, wd_g) = forward_call(
        attn_in, wq4, start, w_out, w_up, w_down
    )
    full_out = wo_g.reshape(D, D)
    full_up = wu_g.reshape(D, -1)
    full_down = wd_g.reshape(-1, D)
    attn_low = o_home.transpose(1, 0, 2).reshape(rows, D)
    attn_branch = dot_nn(attn_low, full_out)
    middle = inputs32 + attn_branch
    norm_two, inverse_two = normalize(middle)
    mlp_in = (norm_two * gain_mlp).astype(BF)
    up_proj = dot_nn(mlp_in, full_up)
    activated = gelu_tanh(up_proj).astype(BF)
    mlp_branch = dot_nn(activated, full_down)
    output = (middle + mlp_branch).astype(BF)
    squares = jnp.stack(
        [jnp.sum(t * t) for t in (inputs32, attn_branch, middle, mlp_branch)]
    )
    d_act = dot_nt(d_output, full_down)
    d_w_down = dot_tn(activated, d_output).astype(BF)
    d_up = jax.vjp(gelu_tanh, up_proj)[1](d_act)[0].astype(BF)
    d_w_up = dot_tn(mlp_in, d_up).astype(BF)
    d_mlp_in = dot_nt(d_up, full_up)
    d_middle = d_output.astype(F32) + norm_back(d_mlp_in * gain_mlp, norm_two, inverse_two)
    g_middle = d_middle.astype(BF)
    d_w_out = dot_tn(attn_low, g_middle).astype(BF)
    d_attn = dot_nt(g_middle, full_out).astype(BF)
    dah = d_attn.reshape(rows, SPAN, WIDE).transpose(1, 0, 2)
    extra = jnp.zeros((SPAN, D // 12, D), BF)
    extra = extra.at[:, 0, 0].set(squares.astype(BF))
    go = jnp.concatenate([d_w_out.reshape(SPAN, D // SPAN, D), extra], axis=1)
    dxh, fd, fu, fo, fq = backward_call(
        dah, xg, wq, q, k, v, ah, tot, starts,
        d_w_down.reshape(SPAN, -1, D), d_w_up.reshape(SPAN, D // SPAN, -1), go,
    )
    d_attn_in = (dxh[0].astype(F32) + dxh[1].astype(F32)).reshape(rows, D)
    d_input = d_middle + norm_back(d_attn_in * gain_attn, norm_one, inverse_one)
    total_down = fd.astype(F32)
    total_up = fu.astype(F32)
    total_out = fo[: D // SPAN].astype(F32)
    total_qkv = (
        fq.reshape(SPAN, D // SPAN, 3, WIDE).transpose(1, 2, 0, 3).reshape(D // SPAN, 3 * D).astype(F32)
    )

    def gain_grad(weight, grad, gain):
        own = lax.dynamic_slice_in_dim(gain, kv_index * (D // SPAN), D // SPAN)
        return jnp.sum(weight.astype(F32) * grad, axis=1) / own

    total_gain_attn = gain_grad(w_qkv, total_qkv, gain_attn)
    total_gain_mlp = gain_grad(w_up, total_up, gain_mlp)
    entry_count = rows * SPAN * lax.axis_size("pb") * D
    rms = jnp.sqrt(fo[D // SPAN, 0:1].astype(F32) / entry_count)
    return (
        output, d_input, total_gain_attn, total_qkv, total_out, total_gain_mlp, total_up, total_down, rms,
    )


def solution(mesh):
    if mesh.shape["ka"] != SPAN or mesh.shape["pb"] % 8:
        raise ValueError("unsupported mesh")
    placed = (
        P(("pb", "ka"), None), P("pb"), P(), P("ka", None), P("ka", None), P(), P("ka", None), P("ka", None),
        P(("pb", "ka"), None),
    )
    return jax.shard_map(
        body,
        mesh=mesh,
        in_specs=placed,
        out_specs=(
            P(("pb", "ka"), None), P(("pb", "ka"), None), P("ka"), P("ka", None), P("ka", None), P("ka"),
            P("ka", None), P("ka", None), P("ka"),
        ),
        check_vma=False,
    )
```

time: 443 us -> 349 us (0.79)
  Pallas kernels: 361 us -> 269 us
    pallas_call x2 -> x1, Pallas kernels: 218 us -> 142 us  [backward_call(): pl.pallas_call(functools.partial(backward_kernel, outer), out_shape=(shap...]
    pallas_call x1, Pallas kernels: 143 us -> 128 us  [forward_call(): pl.pallas_call(forward_kernel, out_shape=outs, in_specs=[vmem, anyspace,...]
where the time goes in v3:
time: 349 us; the launch traced here: 346 us
  Pallas kernels  269 us (77%)
  matrix products  33.3 us (10%)
  local copies, waits for them, and re-layouts  20.6 us (6%)
  other arithmetic  18.6 us (5%)
  between operations  3.86 us (1%)
    pallas_call x1, Pallas kernels, backward_call(): pl.pallas_call(functools.partial(backward_kernel, outer), out_shape=(shap...  142 us
    pallas_call x1, Pallas kernels, forward_call(): pl.pallas_call(forward_kernel, out_shape=outs, in_specs=[vmem, anyspace,...  128 us
    dot_general x3, matrix products, dot_nt(): lax.dot_general(left, right, (((1,), (1,)), ((), ())), preferred_element_...  11.4 us
    dot_general x3, matrix products, dot_nn(): return jnp.dot(left, right, preferred_element_type=F32)  11.3 us
    dot_general x3, matrix products, dot_tn(): lax.dot_general(left, right, (((0,), (0,)), ((), ())), preferred_element_...  10.7 us

profile of v3, /device:TPU:0, one launch (start us, length us, event | category | flops | bytes accessed | tf_op | source)
XLA Modules:
  0.0 345.9 jit_solution(5091459642147495184)
XLA Ops:
  1.4 1.4 convert_reduce_fusion
  2.8 2.2 fusion.22
  5.6 1.2 fusion.16.xa
  6.8 1.1 reshape.194
  7.9 1.0 copy.39
  8.9 1.3 copy.40.wq4
  10.3 127.8 %forward_attention.1 = (bf16[4,512,192]{2,1,0:T(8,128)(2,1)}, bf16[4,2,256,768]{3,2,1,0:T(8,128)(2,1)}, bf16[4,192,576]{2,1,0:T(8,128)(2,1)}, bf16[3,2048,64]{2,...) custom-call(bf16[512,768]{1,0:T(8,128)(2,1)} %fusion.16.xa, ...), custom_call_target="tpu_custom_call" | custom-call | tf_op jit(solution)/shard_map/forward_attention/pallas_call | solution.py:452
  138.1 1.5 copy.45
  139.7 3.0 fusion.31
  143.4 2.7 fusion.29
  146.1 6.2 %fusion.6 = bf16[512,3072]{1,0:T(8,128)(2,1)S(1)} fusion(f32[512,3072]{1,0:T(8,128)S(1)} %fusion.29, bf16[3072,768]{1,0:T(8,128)(2,1)S(1)} %bitcast.77, bf16[512,768]{1,0:T(8,128)(2,1)S(1)} %copy-done.13), kind=kOutput, calls=%fused_computation.8 | convolution fusion | flops 2447376384 | bytes 14942208 | tf_op jit(solution)/shard_map/dot_general | solution.py:52
  152.3 3.5 %multiply_reduce_fusion.4 = (bf16[]{:T(256)}, f32[512]{0:T(512)S(1)}, f32[512]{0:T(512)S(1)}, f32[512,768]{1,0:T(8,128)S(1)}) fusion(f32[512,768]{1,0:T(8,128)S(1)} %get-tuple-element.63, f32[512]{0:T(512)S(1)} %add_rsqrt_fusion, f32[512]{0:T(512)S(1)} %broadcast_multiply_fusion.3, f32[768]{0:T(1024)S(1)} %copy-done.10, bf16[512,3072]{1,0:T(8,128)(2,1)S(1)} %fusion.6, ...), kind=kOutput, calls=%fused_computation.44 | convolution fusion | flops 2419063808 | bytes 11021314 | tf_op jit(solution)/shard_map/dot_general | solution.py:52
  155.8 5.6 %multiply_reduce_fusion.3 = (bf16[]{:T(256)}, bf16[512,768]{1,0:T(8,128)(2,1)}, f32[512,768]{1,0:T(8,128)S(1)}) fusion(f32[512,768]{1,0:T(8,128)S(1)} %get-tuple-element.63, f32[512]{0:T(512)S(1)} %get-tuple-element.71, f32[512]{0:T(512)S(1)} %broadcast_multiply_fusion.3, f32[512,768]{1,0:T(8,128)S(1)} %get-tuple-element.70, f32[512]{0:T(512)S(1)} %get-tuple-element.72, ...), kind=kOutput, calls=%fused_computation.43 | convolution fusion | flops 2434793472 | bytes 17309698 | tf_op jit(solution)/shard_map/dot_general | solution.py:60
  161.4 5.1 %convolution_convert_fusion.1 = bf16[3072,768]{1,0:T(8,128)(2,1)} fusion(bf16[512,768]{1,0:T(8,128)(2,1)S(1)} %copy-done.13, f32[512,3072]{1,0:T(8,128)S(1)} %fusion.29), kind=kOutput, calls=%fused_computation.16 | convolution fusion | flops 2432434176 | bytes 11796480 | tf_op jit(solution)/shard_map/dot_general | solution.py:56
  166.5 4.8 %convolution_convert_fusion = bf16[768,3072]{1,0:T(8,128)(2,1)} fusion(bf16[512,3072]{1,0:T(8,128)(2,1)S(1)} %fusion.6, f32[512,768]{1,0:T(8,128)S(1)} %get-tuple-element.63, f32[768]{0:T(1024)S(1)} %copy-done.10, f32[512]{0:T(512)S(1)} %add_rsqrt_fusion, f32[512]{0:T(512)S(1)} %broadcast_multiply_fusion.3), kind=kOutput, calls=%fused_computation.15 | convolution fusion | flops 2419851264 | bytes 9444352 | tf_op jit(solution)/shard_map/dot_general | solution.py:56
  171.3 2.7 pad_maximum_fusion
  173.9 1.7 convolution_convert_fusion.3
  175.6 2.3 copy.43
  178.0 2.2 copy.44
  181.0 1.3 fusion.23.go
  182.3 141.7 %backward_attention.1 = (bf16[2,2,256,768]{3,2,1,0:T(8,128)(2,1)}, bf16[768,768]{1,0:T(8,128)(2,1)}, bf16[192,3072]{1,0:T(8,128)(2,1)}, bf16[256,768]{1,0:T(8,128)(2,1)}, bf16[4,192,576]{2,1,0:T(8,128)(2,1)}) custom-call(bf16[4,512,192]{2,1,0:T(8,128)(2,1)} %bitcast.70, bf16[4,2,256,768]{3,2,1,0:T(8,128)(2,1)} %get-tuple-element.42.xg_in, ...), custom_call_target="tpu_custom_call" | custom-call | tf_op jit(solution)/shard_map/backward_attention/pallas_call | solution.py:956
  324.0 1.2 slice.34
  325.8 1.7 multiply_reduce_fusion.2
  328.1 1.7 fusion.20
  329.8 0.9 slice_convert_fusion
  330.7 1.5 copy.47
  332.2 2.5 copy.48
  334.7 2.9 reshape.204
  338.5 1.0 copy-done.6
  339.5 1.6 convert_element_type.115
  341.2 0.8 copy-done.5
  342.0 1.7 multiply_reduce_fusion
  (47 shorter events, 4.4 us)
Async XLA Ops:
  0.6 5.0 %copy-start = (bf16[512,768]{1,0:T(8,128)(2,1)S(1)}, bf16[512,768]{1,0:T(8,128)(2,1)}, u32[]{:S(2)}) copy-start(bf16[512,768]{1,0:T(8,128)(2,1)} %param.11) | copy-start | bytes 2359300
  0.7 5.0 %copy-start.9 = (f32[768]{0:T(1024)S(1)}, f32[768]{0:T(1024)}, u32[]{:S(2)}) copy-start(f32[768]{0:T(1024)} %param.13) | copy-start | bytes 9220
  1.4 5.4 %copy-start.3 = (bf16[192,2304]{1,0:T(8,128)(2,1)S(1)}, bf16[192,2304]{1,0:T(8,128)(2,1)}, u32[]{:S(2)}) copy-start(bf16[192,2304]{1,0:T(8,128)(2,1)} %param.14) | copy-start | bytes 2654212
  138.1 1.6 copy-start.7
  139.7 3.3 copy-start.11
  142.7 0.7 copy-start.10
  142.7 3.4 slice-start
  143.3 2.8 slice-start.1
  143.3 2.8 copy-start.13
  166.5 7.4 %copy-start.12 = (bf16[4,192,768]{2,1,0:T(8,128)(2,1)S(1)}, bf16[4,192,768]{2,1,0:T(8,128)(2,1)}, u32[]{:S(2)}) copy-start(bf16[4,192,768]{2,1,0:T(8,128)(2,1)} %get-tuple-element.39) | copy-start | bytes 3538948
  328.1 1.7 copy-start.8
  334.7 2.9 copy-start.4
  337.6 3.5 %copy-start.1 = (f32[192,2304]{1,0:T(8,128)}, f32[192,2304]{1,0:T(8,128)S(1)}, u32[]{:S(2)}) copy-start(f32[192,2304]{1,0:T(8,128)S(1)} %reshape.204) | copy-start | bytes 5308420
  337.6 1.9 copy-start.6
  339.5 1.7 copy-start.2
  339.5 2.5 copy-start.5
